TPU v7x, 32 devices: a whole 2x2x4 slice. The times are simulated.
32 devices in a mesh: groups: 2 (over y), tile: 4 (over z), image: 4 (over x, core).
Axes of the slice: x: 2, y: 2, z: 4, core: 2. Of those that a mesh axis runs over, the one named last changes fastest.
Arguments:
- images: bfloat16 [8, 16, 64, 256], P(('groups', 'image'), 'tile'), parts along dimension 0, may hold values from -12 to 12
- cotangent: bfloat16 [8, 16, 64, 256], P(('groups', 'image'), 'tile'), parts along dimension 0, may hold values from -12 to 12
- timesteps: int32 [8], P(('groups', 'image')), parts along dimension 0, may hold values from 0 to 999
- class_ids: int32 [8], P(('groups', 'image')), parts along dimension 0, may hold values from 0 to 999
- norm_gain: float32 [256], replicated, may hold values from 0.25 to 1.75
- norm_bias: float32 [256], replicated, may hold values from -3 to 3
- conv_first: bfloat16 [3, 3, 256, 256], replicated, may hold values from -0.125 to 0.125
- conv_second: bfloat16 [3, 3, 256, 256], replicated, may hold values from -0.125 to 0.125
- time_weight: bfloat16 [256, 1024], P(None, 'tile'), may hold values from -0.375 to 0.375
- time_bias: float32 [1024], P('tile'), may hold values from -3 to 3
- class_table: bfloat16 [1000, 1024], P(None, 'tile'), may hold values from -5 to 5
- adaptive_weight: bfloat16 [1024, 512], P('tile'), may hold values from -0.1875 to 0.1875
- adaptive_bias: float32 [512], replicated, may hold values from -2 to 2
Outputs:
- branch: bfloat16 [8, 16, 64, 256], P(('groups', 'image'), 'tile'), parts along dimension 0
- input_grad: bfloat16 [8, 16, 64, 256], P(('groups', 'image'), 'tile'), parts along dimension 0
- grad_adaptive_weight: float32 [2048, 512], P(('groups', 'tile')), parts along dimension 0
- grad_adaptive_bias: float32 [1024], P('groups'), parts along dimension 0
There are 2 independent parts, one for each index of `groups`. A program takes and returns all parts, laid end to end along the dimension named above; an argument that names none is the same for every part. Nothing has to cross between parts.
All inputs are finite; a program needn't handle non-finite values.
Results may differ from a plain program's by a relative error of at most 0.013.
Values may be sent and summed in bfloat16 or wider, within the bound.
A program may use at most 64 MiB of HBM per device.

v0:
```python
import functools
import math

import jax
import jax.numpy as jnp
from jax import lax
from jax.experimental import pallas as pl
from jax.experimental.pallas import tpu as pltpu
from jax.sharding import PartitionSpec as P

GN_GROUPS = 32
EPSILON = 1e-05
MESH = pl.DeviceIdType.MESH
F32 = jnp.float32
BF16 = jnp.bfloat16
GRANT = 24 << 20
REACH = 2
HIGHEST = lax.Precision.HIGHEST


def group_spread(values, width):
    count = values.shape[-1]
    lane = lax.broadcasted_iota(jnp.int32, values.shape, values.ndim - 1)
    step = 1
    while step < width:
        up = pltpu.roll(values, step, values.ndim - 1)
        down = pltpu.roll(values, count - step, values.ndim - 1)
        values = values + jnp.where((lane & step) != 0, up, down)
        step *= 2
    return values


def silu_slope(pre, sigma):
    return sigma * (1.0 + pre * (1.0 - sigma))


def column_sums(first, second):
    return jnp.concatenate(
        [jnp.sum(first, axis=0, keepdims=True), jnp.sum(second, axis=0, keepdims=True)], axis=0
    )


def kernel(
    n, m,
    steps_ref, ids_ref, gain_hbm, bias_hbm, tbias_hbm, abias_hbm,
    images_hbm, cot_hbm, first_hbm, second_hbm, tweight_hbm, table_hbm, aweight_hbm,
    branch, igrad, wgrad, bgrad,
    images, cot, first, second, tweight, table, aweight,
    gain_ref, bias_ref, tbias_ref, abias_ref,
    wide_first, wide_cot, wide_second, wide_hidden,
    hidden, gact, nsecond, gpre, nfirst, slope,
    slots, acts, pairs,
    load_sem, halo_send, halo_recv, send_sem, recv_sem,
    act_send, act_recv, pair_send, pair_recv,
):
    me = lax.axis_index("tile")
    mine = lax.axis_index("image")
    rows, cols, channels = images_hbm.shape[1:]
    width = channels // GN_GROUPS
    cells = float(rows * cols * n * width)
    own = rows * cols
    rim = cols
    above, below = me > 0, me < n - 1

    loads = [
        pltpu.make_async_copy(source, target, load_sem.at[k])
        for k, (source, target) in enumerate(
            [
                (images_hbm.at[0], images.at[pl.ds(REACH, rows)]),
                (cot_hbm.at[0], cot.at[pl.ds(REACH, rows)]),
                (tweight_hbm, tweight),
                (table_hbm, table),
                (aweight_hbm, aweight),
                (first_hbm, first),
                (second_hbm, second),
                (gain_hbm, gain_ref),
                (bias_hbm, bias_ref),
                (tbias_hbm, tbias_ref),
                (abias_hbm, abias_ref),
            ]
        )
    ]
    for load in loads:
        load.start()

    barrier = pltpu.get_barrier_semaphore()
    for k in range(1, n):
        pl.semaphore_signal(
            barrier, inc=1, device_id={"tile": lax.rem(me + k, n)}, device_id_type=MESH
        )
    for k in range(1, m):
        pl.semaphore_signal(
            barrier, inc=1, device_id={"image": lax.rem(mine + k, m)}, device_id_type=MESH
        )

    def tile_copy(stage, k, arriving):
        peer = lax.rem(me + k, n)
        slot = lax.rem(me + n - k, n) if arriving else me
        return pltpu.make_async_remote_copy(
            src_ref=slots.at[stage, slot],
            dst_ref=slots.at[stage, slot],
            send_sem=send_sem.at[stage, k],
            recv_sem=recv_sem.at[stage, k],
            device_id={"tile": peer},
            device_id_type=MESH,
        )

    def share(stage, value):
        slots[stage, me] = value
        for k in range(1, n):
            tile_copy(stage, k, False).start()

    def total(stage):
        for k in range(1, n):
            tile_copy(stage, k, True).wait_recv()
        summed = slots[stage, 0]
        for k in range(1, n):
            summed = summed + slots[stage, k]
        return summed

    def image_copy(buffer, sends, receives, k, arriving):
        peer = lax.rem(mine + k, m)
        slot = lax.rem(mine + m - k, m) if arriving else mine
        return pltpu.make_async_remote_copy(
            src_ref=buffer.at[slot],
            dst_ref=buffer.at[slot],
            send_sem=sends.at[k],
            recv_sem=receives.at[k],
            device_id={"image": peer},
            device_id_type=MESH,
        )

    def halo_copy(which, buffer, up):
        source = pl.ds(REACH, REACH) if up else pl.ds(rows, REACH)
        target = pl.ds(rows + REACH, REACH) if up else pl.ds(0, REACH)
        return pltpu.make_async_remote_copy(
            src_ref=buffer.at[source],
            dst_ref=buffer.at[target],
            send_sem=halo_send.at[which, int(up)],
            recv_sem=halo_recv.at[which, int(up)],
            device_id={"tile": me - 1 if up else me + 1},
            device_id_type=MESH,
        )

    def flat(buffer, start, count):
        return buffer[pl.ds(start, count)].reshape(count * cols, channels).astype(F32)

    def widen(wide, start, values):
        count = values.shape[0]
        column = lax.rem(lax.broadcasted_iota(jnp.int32, values.shape, 0), cols)
        before = jnp.where(column == 0, 0.0, pltpu.roll(values, 1, 0))
        after = jnp.where(column == cols - 1, 0.0, pltpu.roll(values, count - 1, 0))
        at = pl.ds(start * cols, count)
        wide[at, 0:channels] = before.astype(BF16)
        wide[at, channels : 2 * channels] = values.astype(BF16)
        wide[at, 2 * channels : 3 * channels] = after.astype(BF16)

    def conv(wide, start, count, weight):
        summed = None
        for i in range(3):
            product = jnp.dot(
                wide[pl.ds((start + i) * cols, count * cols), :],
                weight[i].reshape(3 * channels, channels),
                preferred_element_type=F32,
            )
            summed = product if summed is None else summed + product
        return summed

    def conv_back(wide, start, count, weight):
        summed = None
        for i in range(3):
            for j in range(3):
                product = lax.dot_general(
                    wide[pl.ds((start + i) * cols, count * cols), j * channels : (j + 1) * channels],
                    weight[2 - i, 2 - j],
                    (((1,), (1,)), ((), ())),
                    preferred_element_type=F32,
                )
                summed = product if summed is None else summed + product
        return summed

    def moments(summed):
        spread = group_spread(summed, width) / cells
        centre = spread[0:1]
        variance = jnp.maximum(spread[1:2] - centre * centre, 0.0)
        return centre, lax.rsqrt(variance + EPSILON)

    loads[0].wait()
    values = flat(images, REACH, rows)
    sums = column_sums(values, values * values)
    pl.semaphore_wait(barrier, n - 1 + m - 1)
    share(0, sums)
    def halo_start(which, buffer):

        @pl.when(above)
        def _():
            halo_copy(which, buffer, True).start()

        @pl.when(below)
        def _():
            halo_copy(which, buffer, False).start()

        @pl.when(jnp.logical_not(above))
        def _():
            buffer[pl.ds(0, REACH)] = jnp.zeros((REACH, cols, channels), BF16)

        @pl.when(jnp.logical_not(below))
        def _():
            buffer[pl.ds(rows + REACH, REACH)] = jnp.zeros((REACH, cols, channels), BF16)

    halo_start(0, images)

    for k in (2, 3, 4, 7, 8, 9, 10):
        loads[k].wait()
    half = tweight.shape[0] // 2
    index = lax.broadcasted_iota(jnp.int32, (half, 1), 0).astype(F32)
    angles = steps_ref[0].astype(F32) * jnp.exp(-math.log(10000.0) * index / half)
    pre_time = (
        jnp.sum(jnp.cos(angles) * tweight[0:half].astype(F32), axis=0, keepdims=True)
        + jnp.sum(jnp.sin(angles) * tweight[half:].astype(F32), axis=0, keepdims=True)
        + tbias_ref[...]
    )
    entry = lax.broadcasted_iota(jnp.int32, table.shape, 0) == ids_ref[0]
    picked = jnp.sum(jnp.where(entry, table[...].astype(F32), 0.0), axis=0, keepdims=True)
    embedding = pre_time * jax.nn.sigmoid(pre_time) + picked
    activated = embedding * jax.nn.sigmoid(embedding)
    acts[mine] = activated
    for k in range(1, m):
        image_copy(acts, act_send, act_recv, k, False).start()
    partial = jnp.dot(
        jnp.broadcast_to(activated, (8, activated.shape[1])),
        aweight[...].astype(F32),
        precision=HIGHEST,
        preferred_element_type=F32,
    )[0:1]
    share(1, jnp.concatenate([partial[:, :channels], partial[:, channels:]], axis=0))

    loads[1].wait()
    halo_start(1, cot)

    gain, bias = gain_ref[...], bias_ref[...]
    centre, inverse_first = moments(total(0))

    def first_activation(normed):
        pre = normed * gain + bias
        return pre, jax.nn.sigmoid(pre)

    values = (flat(images, REACH, rows) - centre) * inverse_first
    pre, sigma = first_activation(values)
    widen(wide_first, REACH, pre * sigma)

    def halo_wait(which, buffer):
        @pl.when(below)
        def _():
            halo_copy(which, buffer, True).wait_recv()

        @pl.when(above)
        def _():
            halo_copy(which, buffer, False).wait_recv()

    halo_wait(0, images)
    for start, inside in ((0, above), (rows + REACH, below)):
        rim_values = (flat(images, start, REACH) - centre) * inverse_first
        rim_pre, rim_sigma = first_activation(rim_values)
        widen(wide_first, start, jnp.where(inside, rim_pre * rim_sigma, 0.0))
    loads[5].wait()
    centre_rows = conv(wide_first, 1, rows, first).astype(BF16).astype(F32)
    share(2, column_sums(centre_rows, centre_rows * centre_rows))
    hidden[pl.ds(rim, own)] = centre_rows

    for row in (0, rows + 1):
        hidden[pl.ds(row * cols, cols)] = conv(wide_first, row, 1, first).astype(BF16).astype(F32)
    halo_wait(1, cot)
    widen(wide_cot, 0, flat(cot, 0, rows + 2 * REACH))
    loads[6].wait()
    gact[...] = conv_back(wide_cot, 0, rows + 2, second)
    values = (flat(images, REACH, rows) - centre) * inverse_first
    pre, sigma = first_activation(values)
    nfirst[...] = values
    slope[...] = silu_slope(pre, sigma) * gain

    modulation = total(1)
    factor = 1.0 + (modulation[0:1] + abias_ref[:, :channels])
    shift = modulation[1:2] + abias_ref[:, channels:]
    centre, inverse_second = moments(total(2))
    for start, count, inside in ((1, rows, None), (0, 1, above), (rows + 1, 1, below)):
        at = pl.ds(start * cols, count * cols)
        normed = (hidden[at] - centre) * inverse_second
        pre = normed * factor + shift
        sigma = jax.nn.sigmoid(pre)
        back = gact[at] * silu_slope(pre, sigma)
        if inside is None:
            share(3, column_sums(back * normed, back))
        active = pre * sigma
        if inside is not None:
            active = jnp.where(inside, active, 0.0)
        widen(wide_second, start, active)
        nsecond[at] = normed
        gpre[at] = back

    branch[0] = conv(wide_second, 0, rows, second).astype(BF16).reshape(rows, cols, channels)

    sums = total(3)
    spread = group_spread(sums * factor, width) / cells
    paired_mean, plain_mean = spread[0:1], spread[1:2]
    for start, count, inside in ((1, rows, None), (0, 1, above), (rows + 1, 1, below)):
        at = pl.ds(start * cols, count * cols)
        back = inverse_second * (gpre[at] * factor - plain_mean - nsecond[at] * paired_mean)
        if inside is not None:
            back = jnp.where(inside, back, 0.0)
        widen(wide_hidden, start, back)
    pairs[mine] = sums
    for k in range(1, m):
        image_copy(pairs, pair_send, pair_recv, k, False).start()
    back = conv_back(wide_hidden, 0, rows, first) * slope[...]
    normed = nfirst[...]
    share(4, column_sums(back, back * normed))

    for k in range(1, m):
        image_copy(acts, act_send, act_recv, k, True).wait_recv()
        image_copy(pairs, pair_send, pair_recv, k, True).wait_recv()
    extra = (-m) % 8

    def stacked(pieces):
        if extra:
            pieces = pieces + [jnp.zeros((extra, pieces[0].shape[1]), F32)]
        return jnp.concatenate(pieces, axis=0)

    left = stacked([acts[k] for k in range(m)])
    for part in range(2):
        right = stacked([pairs[k][part : part + 1] for k in range(m)])
        columns = slice(part * channels, (part + 1) * channels)
        wgrad[:, columns] = lax.dot_general(
            left, right, (((0,), (0,)), ((), ())), precision=HIGHEST, preferred_element_type=F32
        )
        bgrad[:, columns] = jnp.sum(right, axis=0, keepdims=True)

    spread = group_spread(total(4), width) / cells
    result = inverse_first * (back - spread[0:1] - normed * spread[1:2])
    igrad[0] = result.astype(BF16).reshape(rows, cols, channels)

    for stage in range(5):
        for k in range(1, n):
            tile_copy(stage, k, False).wait_send()
    for k in range(1, m):
        image_copy(acts, act_send, act_recv, k, False).wait_send()
        image_copy(pairs, pair_send, pair_recv, k, False).wait_send()
    for which, buffer in enumerate((images, cot)):

        @pl.when(above)
        def _():
            halo_copy(which, buffer, True).wait_send()

        @pl.when(below)
        def _():
            halo_copy(which, buffer, False).wait_send()

def finish(*refs):
    count = (len(refs) - 1) // 2
    sem = refs[-1]
    copies = [
        pltpu.make_async_copy(refs[k], refs[count + k], sem.at[k]) for k in range(count)
    ]
    for copy in copies:
        copy.start()
    for copy in copies:
        copy.wait()


def body(
    n, m,
    images, cotangent, timesteps, class_ids, norm_gain, norm_bias, conv_first, conv_second,
    time_weight, time_bias, class_table, adaptive_weight, adaptive_bias,
):
    count, rows, cols, channels = images.shape
    assert count == 1 and rows >= REACH
    emb = time_weight.shape[1]
    vmem = pl.BlockSpec(memory_space=pltpu.VMEM)
    anywhere = pl.BlockSpec(memory_space=pl.ANY)
    padded = rows + 2 * REACH
    own, more, most = rows * cols, (rows + 2) * cols, padded * cols
    dma = pltpu.SemaphoreType.DMA
    results = pl.pallas_call(
        functools.partial(kernel, n, m),
        out_shape=(
            jax.ShapeDtypeStruct(images.shape, BF16),
            jax.ShapeDtypeStruct(images.shape, BF16),
            jax.ShapeDtypeStruct((emb, 2 * channels), F32),
            jax.ShapeDtypeStruct((1, 2 * channels), F32),
        ),
        in_specs=[pl.BlockSpec(memory_space=pltpu.SMEM)] * 2
        + [pl.BlockSpec(memory_space=pltpu.HBM)] * 11,
        out_specs=(vmem,) * 4,
        scratch_shapes=[
            pltpu.VMEM((padded, cols, channels), BF16),
            pltpu.VMEM((padded, cols, channels), BF16),
            pltpu.VMEM(conv_first.shape, BF16),
            pltpu.VMEM(conv_second.shape, BF16),
            pltpu.VMEM(time_weight.shape, BF16),
            pltpu.VMEM(class_table.shape, BF16),
            pltpu.VMEM(adaptive_weight.shape, BF16),
            pltpu.VMEM((1, channels), F32),
            pltpu.VMEM((1, channels), F32),
            pltpu.VMEM((1, emb), F32),
            pltpu.VMEM((1, 2 * channels), F32),
            pltpu.VMEM((most, 3 * channels), BF16),
            pltpu.VMEM((most, 3 * channels), BF16),
            pltpu.VMEM((more, 3 * channels), BF16),
            pltpu.VMEM((more, 3 * channels), BF16),
            pltpu.VMEM((more, channels), F32),
            pltpu.VMEM((more, channels), F32),
            pltpu.VMEM((more, channels), F32),
            pltpu.VMEM((more, channels), F32),
            pltpu.VMEM((own, channels), F32),
            pltpu.VMEM((own, channels), F32),
            pltpu.VMEM((5, n, 2, channels), F32),
            pltpu.VMEM((m, 1, emb), F32),
            pltpu.VMEM((m, 2, channels), F32),
            dma((11,)),
            dma((2, 2)),
            dma((2, 2)),
            dma((5, n)),
            dma((5, n)),
            dma((m,)),
            dma((m,)),
            dma((m,)),
            dma((m,)),
        ],
        compiler_params=pltpu.CompilerParams(
            collective_id=0, has_side_effects=True, vmem_limit_bytes=GRANT
        ),
    )(
        timesteps, class_ids,
        *(
            pltpu.with_memory_space_constraint(operand, pltpu.HBM)
            for operand in (
                norm_gain[None], norm_bias[None], time_bias[None],
                adaptive_bias[None], images, cotangent, conv_first, conv_second, time_weight,
                class_table, adaptive_weight,
            )
        )
    )
    branch, igrad, wgrad, bgrad = pl.pallas_call(
        finish,
        out_shape=tuple(jax.ShapeDtypeStruct(r.shape, r.dtype) for r in results),
        in_specs=[anywhere] * 4,
        out_specs=(anywhere,) * 4,
        scratch_shapes=[dma((4,))],
        compiler_params=pltpu.CompilerParams(vmem_limit_bytes=GRANT),
    )(*results)
    return branch, igrad, wgrad, bgrad[0]


def solution(mesh):
    return jax.shard_map(
        functools.partial(body, mesh.shape["tile"], mesh.shape["image"]),
        mesh=mesh,
        in_specs=(
            P(("groups", "image"), "tile", None, None),
            P(("groups", "image"), "tile", None, None),
            P(("groups", "image")),
            P(("groups", "image")),
            P(),
            P(),
            P(),
            P(),
            P(None, "tile"),
            P("tile"),
            P(None, "tile"),
            P("tile", None),
            P(),
        ),
        out_specs=(
            P(("groups", "image"), "tile", None, None),
            P(("groups", "image"), "tile", None, None),
            P(("groups", "tile"), None),
            P("groups"),
        ),
        check_vma=False,
    )
```

profile of v0, /device:TPU:0, one launch (start us, length us, event | category | flops | bytes accessed | tf_op | source)
XLA Modules:
  0.0 25.7 jit_solution(10996030201594590553)
XLA Ops:
  1.9 22.9 %shard_map.156 = (bf16[1,4,64,256]{3,2,1,0:T(8,128)(2,1)S(1)}, bf16[1,4,64,256]{3,2,1,0:T(8,128)(2,1)S(1)}, f32[256,512]{1,0:T(8,128)S(1)}, f32[1,512]{1,0:T(1,128)S(1)}) custom-call(s32[1]{0:T(128)S(6)} %copy.17.steps_ref, s32[1]{0:T(128)S(6)} %copy.18.ids_ref, f32[1,256]{1,0:T(1,128)} %bitcast.6, f32[1,256]{1,0:T(1,128)} %bitcast.7, f32[1,256]{1,0:T(1,128)} %bitcast.8, ...), custom_call_target="tpu_custom_call" | custom-call | tf_op jit(solution)/shard_map/pallas_call | solution.py:383
  24.8 0.9 %shard_map.157 = (bf16[1,4,64,256]{3,2,1,0:T(8,128)(2,1)}, bf16[1,4,64,256]{3,2,1,0:T(8,128)(2,1)}, f32[256,512]{1,0:T(8,128)}, f32[1,512]{1,0:T(1,128)}) custom-call(bf16[1,4,64,256]{3,2,1,0:T(8,128)(2,1)S(1)} %get-tuple-element.12.refs_0_, bf16[1,4,64,256]{3,2,1,0:T(8,128)(2,1)S(1)} %get-tuple-element.13.refs_1_, ...), custom_call_target="tpu_custom_call" | custom-call | tf_op jit(solution)/shard_map/pallas_call | solution.py:443
where the time goes:
time: 25.9 us; the launch traced here: 25.7 us
  Pallas kernels  23.8 us (92%)
  between operations  1.93 us (7%)
    pallas_call x1, Pallas kernels, body(): pl.pallas_call(functools.partial(kernel, n, m), out_shape=(jax.ShapeDtype...  22.9 us
    pallas_call x1, Pallas kernels, body(): pl.pallas_call(finish, out_shape=tuple((jax.ShapeDtypeStruct(r.shape, r.d...  0.92 us

commit v1 on v0

--- a/solution.py
+++ b/solution.py
@@ -42,11 +42,11 @@
 
 def kernel(
     n, m,
-    steps_ref, ids_ref, gain_hbm, bias_hbm, tbias_hbm, abias_hbm,
+    steps_hbm, ids_hbm, gain_hbm, bias_hbm, tbias_hbm, abias_hbm,
     images_hbm, cot_hbm, first_hbm, second_hbm, tweight_hbm, table_hbm, aweight_hbm,
     branch, igrad, wgrad, bgrad,
     images, cot, first, second, tweight, table, aweight,
-    gain_ref, bias_ref, tbias_ref, abias_ref,
+    gain_ref, bias_ref, tbias_ref, abias_ref, steps_ref, ids_ref,
     wide_first, wide_cot, wide_second, wide_hidden,
     hidden, gact, nsecond, gpre, nfirst, slope,
     slots, acts, pairs,
@@ -77,12 +77,12 @@
                 (bias_hbm, bias_ref),
                 (tbias_hbm, tbias_ref),
                 (abias_hbm, abias_ref),
+                (steps_hbm, steps_ref),
+                (ids_hbm, ids_ref),
             ]
         )
     ]
-    for load in loads:
-        load.start()
-
+    loads[0].start()
     barrier = pltpu.get_barrier_semaphore()
     for k in range(1, n):
         pl.semaphore_signal(
@@ -92,6 +92,8 @@
         pl.semaphore_signal(
             barrier, inc=1, device_id={"image": lax.rem(mine + k, m)}, device_id_type=MESH
         )
+    for load in loads[1:]:
+        load.start()
 
     def tile_copy(stage, k, arriving):
         peer = lax.rem(me + k, n)
@@ -210,17 +212,17 @@
 
     halo_start(0, images)
 
-    for k in (2, 3, 4, 7, 8, 9, 10):
+    for k in (2, 3, 4, 7, 8, 9, 10, 11, 12):
         loads[k].wait()
     half = tweight.shape[0] // 2
     index = lax.broadcasted_iota(jnp.int32, (half, 1), 0).astype(F32)
-    angles = steps_ref[0].astype(F32) * jnp.exp(-math.log(10000.0) * index / half)
+    angles = steps_ref[0, 0].astype(F32) * jnp.exp(-math.log(10000.0) * index / half)
     pre_time = (
         jnp.sum(jnp.cos(angles) * tweight[0:half].astype(F32), axis=0, keepdims=True)
         + jnp.sum(jnp.sin(angles) * tweight[half:].astype(F32), axis=0, keepdims=True)
         + tbias_ref[...]
     )
-    entry = lax.broadcasted_iota(jnp.int32, table.shape, 0) == ids_ref[0]
+    entry = lax.broadcasted_iota(jnp.int32, table.shape, 0) == ids_ref[0, 0]
     picked = jnp.sum(jnp.where(entry, table[...].astype(F32), 0.0), axis=0, keepdims=True)
     embedding = pre_time * jax.nn.sigmoid(pre_time) + picked
     activated = embedding * jax.nn.sigmoid(embedding)
@@ -388,8 +390,7 @@
             jax.ShapeDtypeStruct((emb, 2 * channels), F32),
             jax.ShapeDtypeStruct((1, 2 * channels), F32),
         ),
-        in_specs=[pl.BlockSpec(memory_space=pltpu.SMEM)] * 2
-        + [pl.BlockSpec(memory_space=pltpu.HBM)] * 11,
+        in_specs=[anywhere] * 2 + [pl.BlockSpec(memory_space=pltpu.HBM)] * 11,
         out_specs=(vmem,) * 4,
         scratch_shapes=[
             pltpu.VMEM((padded, cols, channels), BF16),
@@ -403,6 +404,8 @@
             pltpu.VMEM((1, channels), F32),
             pltpu.VMEM((1, emb), F32),
             pltpu.VMEM((1, 2 * channels), F32),
+            pltpu.SMEM((1, 1), jnp.int32),
+            pltpu.SMEM((1, 1), jnp.int32),
             pltpu.VMEM((most, 3 * channels), BF16),
             pltpu.VMEM((most, 3 * channels), BF16),
             pltpu.VMEM((more, 3 * channels), BF16),
@@ -416,7 +419,7 @@
             pltpu.VMEM((5, n, 2, channels), F32),
             pltpu.VMEM((m, 1, emb), F32),
             pltpu.VMEM((m, 2, channels), F32),
-            dma((11,)),
+            dma((13,)),
             dma((2, 2)),
             dma((2, 2)),
             dma((5, n)),
@@ -430,7 +433,7 @@
             collective_id=0, has_side_effects=True, vmem_limit_bytes=GRANT
         ),
     )(
-        timesteps, class_ids,
+        timesteps[None], class_ids[None],
         *(
             pltpu.with_memory_space_constraint(operand, pltpu.HBM)
             for operand in (

time: 25.9 us -> 25.9 us (level)
  no operation moved by 1% of the time
where the time goes in v1:
time: 25.9 us; the launch traced here: 25.7 us
  Pallas kernels  23.8 us (92%)
  between operations  1.93 us (7%)
    pallas_call x1, Pallas kernels, body(): pl.pallas_call(functools.partial(kernel, n, m), out_shape=(jax.ShapeDtype...  22.9 us
    pallas_call x1, Pallas kernels, body(): pl.pallas_call(finish, out_shape=tuple((jax.ShapeDtypeStruct(r.shape, r.d...  0.92 us

profile of v1, /device:TPU:0, one launch (start us, length us, event | category | flops | bytes accessed | tf_op | source)
XLA Modules:
  0.0 25.7 jit_solution(11400127269176749360)
XLA Ops:
  1.9 22.9 %shard_map.156 = (bf16[1,4,64,256]{3,2,1,0:T(8,128)(2,1)S(1)}, bf16[1,4,64,256]{3,2,1,0:T(8,128)(2,1)S(1)}, f32[256,512]{1,0:T(8,128)S(1)}, f32[1,512]{1,0:T(1,128)S(1)}) custom-call(s32[1,1]{1,0:T(1,128)} %bitcast.7.steps_hbm, s32[1,1]{1,0:T(1,128)} %bitcast.8.ids_hbm, f32[1,256]{1,0:T(1,128)} %bitcast.10, f32[1,256]{1,0:T(1,128)} %bitcast.11, ...), custom_call_target="tpu_custom_call" | custom-call | tf_op jit(solution)/shard_map/pallas_call | solution.py:385
  24.8 0.9 %shard_map.157 = (bf16[1,4,64,256]{3,2,1,0:T(8,128)(2,1)}, bf16[1,4,64,256]{3,2,1,0:T(8,128)(2,1)}, f32[256,512]{1,0:T(8,128)}, f32[1,512]{1,0:T(1,128)}) custom-call(bf16[1,4,64,256]{3,2,1,0:T(8,128)(2,1)S(1)} %get-tuple-element.12.refs_0_, bf16[1,4,64,256]{3,2,1,0:T(8,128)(2,1)S(1)} %get-tuple-element.13.refs_1_, ...), custom_call_target="tpu_custom_call" | custom-call | tf_op jit(solution)/shard_map/pallas_call | solution.py:446

commit v2 on v0

--- a/solution.py
+++ b/solution.py
@@ -48,10 +48,11 @@
     images, cot, first, second, tweight, table, aweight,
     gain_ref, bias_ref, tbias_ref, abias_ref,
     wide_first, wide_cot, wide_second, wide_hidden,
+    wide_scaled, wide_plain, tall, table_of,
     hidden, gact, nsecond, gpre, nfirst, slope,
-    slots, acts, pairs,
+    slots, acts, pairs, maps,
     load_sem, halo_send, halo_recv, send_sem, recv_sem,
-    act_send, act_recv, pair_send, pair_recv,
+    act_send, act_recv, pair_send, pair_recv, map_send, map_recv,
 ):
     me = lax.axis_index("tile")
     mine = lax.axis_index("image")
@@ -105,6 +106,31 @@
             device_id_type=MESH,
         )
 
+    def map_copy(k, arriving):
+        slot = lax.rem(me + n - k, n) if arriving else me
+        return pltpu.make_async_remote_copy(
+            src_ref=maps.at[slot],
+            dst_ref=maps.at[slot],
+            send_sem=map_send.at[k],
+            recv_sem=map_recv.at[k],
+            device_id={"tile": lax.rem(me + k, n)},
+            device_id_type=MESH,
+        )
+
+    def pair_copy(k, step, arriving):
+        slot = lax.rem(me + n - k, n) if arriving else me
+        image = lax.rem(mine + m - step, m) if arriving else mine
+        return pltpu.make_async_remote_copy(
+            src_ref=pairs.at[image, slot],
+            dst_ref=pairs.at[image, slot],
+            send_sem=pair_send.at[k, step],
+            recv_sem=pair_recv.at[k, step],
+            device_id={"tile": lax.rem(me + k, n), "image": lax.rem(mine + step, m)},
+            device_id_type=MESH,
+        )
+
+    others = [(k, step) for step in range(m) for k in range(n) if k or step]
+
     def share(stage, value):
         slots[stage, me] = value
         for k in range(1, n):
@@ -178,6 +204,14 @@
                 )
                 summed = product if summed is None else summed + product
         return summed
+
+    def pieces(values):
+        parts = []
+        for _ in range(3):
+            part = values.astype(BF16)
+            parts.append(part)
+            values = values - part.astype(F32)
+        return parts
 
     def moments(summed):
         spread = group_spread(summed, width) / cells
@@ -270,14 +304,86 @@
 
     for row in (0, rows + 1):
         hidden[pl.ds(row * cols, cols)] = conv(wide_first, row, 1, first).astype(BF16).astype(F32)
+
+    values = (flat(images, REACH, rows) - centre) * inverse_first
+    pre, sigma = first_activation(values)
+    nfirst[...] = values
+    steep = silu_slope(pre, sigma) * gain
+    slope[...] = steep
+    edges = []
+    for part, lines in enumerate((steep, steep * values)):
+        lines = lines.astype(BF16).astype(F32)
+        tall[pl.ds(part * channels, channels), :] = lines.T.astype(BF16)
+        by_row = [lines[p * cols : (p + 1) * cols] for p in range(rows)]
+        full = [jnp.sum(line, axis=0, keepdims=True) for line in by_row]
+        kept = [
+            [total_row - line[0:1] for total_row, line in zip(full, by_row)],
+            full,
+            [total_row - line[cols - 1 : cols] for total_row, line in zip(full, by_row)],
+        ]
+        grid = []
+        for i in range(3):
+            for j in range(3):
+                entry = functools.reduce(jnp.add, kept[j])
+                if i == 0:
+                    entry = entry - jnp.where(above, 0.0, kept[j][0])
+                elif i == 2:
+                    entry = entry - jnp.where(below, 0.0, kept[j][rows - 1])
+                grid.append(entry)
+        edges.append(grid)
+    for start, count, inside in ((1, rows, None), (0, 1, above), (rows + 1, 1, below)):
+        lines = hidden[pl.ds(start * cols, count * cols)]
+        if inside is not None:
+            lines = jnp.where(inside, lines, 0.0)
+        widen(wide_plain, start, lines)
+    same = (
+        lax.broadcasted_iota(jnp.int32, (GN_GROUPS, channels), 1) // width
+        == lax.broadcasted_iota(jnp.int32, (GN_GROUPS, channels), 0)
+    )
+    products, constants = [None, None], None
+    for i in range(3):
+        for j in range(3):
+            taps = first[2 - i, 2 - j]
+            wide_taps = taps.astype(F32)
+            near = wide_plain[pl.ds(i * cols, own), j * channels : (j + 1) * channels]
+            for part in range(2):
+                product = wide_taps * jnp.dot(
+                    tall[pl.ds(part * channels, channels), :], near, preferred_element_type=F32
+                )
+                products[part] = product if i + j == 0 else products[part] + product
+            spread_rows = [
+                jnp.where(same, piece.astype(F32), 0.0)
+                for part in range(2)
+                for piece in pieces(edges[part][3 * i + j])
+            ]
+            product = jnp.dot(
+                jnp.concatenate(spread_rows, axis=0).astype(BF16), taps, preferred_element_type=F32
+            )
+            constants = product if i + j == 0 else constants + product
+    blocks = [
+        jnp.sum(product.reshape(GN_GROUPS, width, channels), axis=1) for product in products
+    ] + [
+        sum(constants[(3 * part + q) * GN_GROUPS : (3 * part + q + 1) * GN_GROUPS] for q in range(3))
+        for part in range(2)
+    ]
+    columns_of = [pieces(block) for block in blocks]
+    gathered = None
+    for quarter in range(4):
+        row = lax.broadcasted_iota(jnp.int32, (channels, 4 * GN_GROUPS), 0)
+        lane = lax.broadcasted_iota(jnp.int32, (channels, 4 * GN_GROUPS), 1)
+        chosen = jnp.where(row // width + quarter * GN_GROUPS == lane, 1.0, 0.0).astype(BF16)
+        product = jnp.dot(
+            jnp.concatenate(columns_of[quarter], axis=0), chosen, preferred_element_type=F32
+        )
+        gathered = product if gathered is None else gathered + product
+    maps[me] = sum(gathered[q * GN_GROUPS : (q + 1) * GN_GROUPS] for q in range(3))
+    for k in range(1, n):
+        map_copy(k, False).start()
+
     halo_wait(1, cot)
     widen(wide_cot, 0, flat(cot, 0, rows + 2 * REACH))
     loads[6].wait()
     gact[...] = conv_back(wide_cot, 0, rows + 2, second)
-    values = (flat(images, REACH, rows) - centre) * inverse_first
-    pre, sigma = first_activation(values)
-    nfirst[...] = values
-    slope[...] = silu_slope(pre, sigma) * gain
 
     modulation = total(1)
     factor = 1.0 + (modulation[0:1] + abias_ref[:, :channels])
@@ -290,61 +396,118 @@
         sigma = jax.nn.sigmoid(pre)
         back = gact[at] * silu_slope(pre, sigma)
         if inside is None:
-            share(3, column_sums(back * normed, back))
+            pairs[mine, me] = column_sums(back * normed, back)
+            for k, step in others:
+                pair_copy(k, step, False).start()
         active = pre * sigma
+        back = back * (factor * inverse_second)
         if inside is not None:
             active = jnp.where(inside, active, 0.0)
+            back = jnp.where(inside, back, 0.0)
+        widen(wide_scaled, start, back)
         widen(wide_second, start, active)
         nsecond[at] = normed
         gpre[at] = back
 
+    early = conv_back(wide_scaled, 0, rows, first) * slope[...]
+    share(3, column_sums(early, early * nfirst[...]))
+
     branch[0] = conv(wide_second, 0, rows, second).astype(BF16).reshape(rows, cols, channels)
 
-    sums = total(3)
-    spread = group_spread(sums * factor, width) / cells
-    paired_mean, plain_mean = spread[0:1], spread[1:2]
+    for k in range(1, n):
+        map_copy(k, True).wait_recv()
+    summed = maps[0]
+    for k in range(1, n):
+        summed = summed + maps[k]
+    lanes = 4 * GN_GROUPS
+    spread_of = jnp.where(same, 1.0, 0.0)
+    for q, piece in enumerate(pieces(summed)):
+        table_of[pl.ds(q * lanes, lanes), :] = lax.dot_general(
+            piece.astype(F32), spread_of, (((0,), (0,)), ((), ())), preferred_element_type=F32
+        ).astype(BF16)
+
+    for k in range(1, n):
+        pair_copy(k, 0, True).wait_recv()
+
+    def whole(image):
+        summed = pairs[image, 0]
+        for k in range(1, n):
+            summed = summed + pairs[image, k]
+        return summed
+
+    spread = group_spread(whole(mine) * factor, width) / cells
+    paired_mean, plain_mean = inverse_second * spread[0:1], inverse_second * spread[1:2]
     for start, count, inside in ((1, rows, None), (0, 1, above), (rows + 1, 1, below)):
         at = pl.ds(start * cols, count * cols)
-        back = inverse_second * (gpre[at] * factor - plain_mean - nsecond[at] * paired_mean)
+        back = gpre[at] - plain_mean - nsecond[at] * paired_mean
         if inside is not None:
             back = jnp.where(inside, back, 0.0)
         widen(wide_hidden, start, back)
-    pairs[mine] = sums
-    for k in range(1, m):
-        image_copy(pairs, pair_send, pair_recv, k, False).start()
+
+    tilt = paired_mean * inverse_second
+    level = plain_mean - tilt * centre
+    row = lax.broadcasted_iota(jnp.int32, (channels, lanes), 0)
+    lane = lax.broadcasted_iota(jnp.int32, (channels, lanes), 1)
+    chosen = jnp.where(lax.rem(lane, GN_GROUPS) * width == row, 1.0, 0.0).astype(BF16)
+    short = [piece.astype(F32) for piece in pieces(level) + pieces(tilt)]
+    short = jnp.concatenate(short + [jnp.zeros((2, channels), F32)], axis=0).astype(BF16)
+    short = jnp.dot(short, chosen, preferred_element_type=F32)
+    quarter = lax.broadcasted_iota(jnp.int32, (1, lanes), 1) // GN_GROUPS
+    nothing = jnp.zeros((1, lanes), F32)
+    left = []
+    for part in range(2):
+        mixed = [
+            jnp.where(quarter == part, short[3 + q : 4 + q], jnp.where(quarter == part + 2, short[q : q + 1], 0.0))
+            for q in range(3)
+        ]
+        left += [
+            jnp.concatenate([mixed[q]] * (3 - q) + [nothing] * q, axis=1) for q in range(3)
+        ]
+    left = jnp.concatenate(left + [jnp.zeros((2, 3 * lanes), F32)], axis=0).astype(BF16)
+    moved = jnp.dot(left, table_of[...], preferred_element_type=F32)
+    moved = jnp.concatenate(
+        [jnp.sum(moved[3 * part : 3 * part + 3], axis=0, keepdims=True) for part in range(2)], axis=0
+    )
+
     back = conv_back(wide_hidden, 0, rows, first) * slope[...]
-    normed = nfirst[...]
-    share(4, column_sums(back, back * normed))
+    spread = (group_spread(total(3), width) - moved) / cells
+    result = inverse_first * (back - spread[0:1] - nfirst[...] * spread[1:2])
+    igrad[0] = result.astype(BF16).reshape(rows, cols, channels)
 
     for k in range(1, m):
         image_copy(acts, act_send, act_recv, k, True).wait_recv()
-        image_copy(pairs, pair_send, pair_recv, k, True).wait_recv()
-    extra = (-m) % 8
-
-    def stacked(pieces):
+    for k, step in others:
+        if step:
+            pair_copy(k, step, True).wait_recv()
+    sums = [whole(k) for k in range(m)]
+    extra = (-6 * m) % 16
+
+    def stacked(parts):
         if extra:
-            pieces = pieces + [jnp.zeros((extra, pieces[0].shape[1]), F32)]
-        return jnp.concatenate(pieces, axis=0)
-
-    left = stacked([acts[k] for k in range(m)])
+            parts = parts + [jnp.zeros((extra, parts[0].shape[1]), F32)]
+        return jnp.concatenate(parts, axis=0).astype(BF16)
+
+    thirds = [[piece.astype(F32) for piece in pieces(acts[k])] for k in range(m)]
+    left = stacked([thirds[k][q] for q in (0, 0, 1, 0, 1, 2) for k in range(m)])
     for part in range(2):
-        right = stacked([pairs[k][part : part + 1] for k in range(m)])
+        lines = [value[part : part + 1] for value in sums]
+        thirds = [[piece.astype(F32) for piece in pieces(line)] for line in lines]
+        right = stacked([thirds[k][q] for q in (0, 1, 0, 2, 1, 0) for k in range(m)])
         columns = slice(part * channels, (part + 1) * channels)
         wgrad[:, columns] = lax.dot_general(
-            left, right, (((0,), (0,)), ((), ())), precision=HIGHEST, preferred_element_type=F32
-        )
-        bgrad[:, columns] = jnp.sum(right, axis=0, keepdims=True)
-
-    spread = group_spread(total(4), width) / cells
-    result = inverse_first * (back - spread[0:1] - normed * spread[1:2])
-    igrad[0] = result.astype(BF16).reshape(rows, cols, channels)
-
-    for stage in range(5):
+            left, right, (((0,), (0,)), ((), ())), preferred_element_type=F32
+        )
+        bgrad[:, columns] = functools.reduce(jnp.add, lines)
+
+    for stage in range(4):
         for k in range(1, n):
             tile_copy(stage, k, False).wait_send()
+    for k in range(1, n):
+        map_copy(k, False).wait_send()
     for k in range(1, m):
         image_copy(acts, act_send, act_recv, k, False).wait_send()
-        image_copy(pairs, pair_send, pair_recv, k, False).wait_send()
+    for k, step in others:
+        pair_copy(k, step, False).wait_send()
     for which, buffer in enumerate((images, cot)):
 
         @pl.when(above)
@@ -407,24 +570,31 @@
             pltpu.VMEM((most, 3 * channels), BF16),
             pltpu.VMEM((more, 3 * channels), BF16),
             pltpu.VMEM((more, 3 * channels), BF16),
+            pltpu.VMEM((more, 3 * channels), BF16),
+            pltpu.VMEM((more, 3 * channels), BF16),
+            pltpu.VMEM((2 * channels, own), BF16),
+            pltpu.VMEM((12 * GN_GROUPS, channels), BF16),
             pltpu.VMEM((more, channels), F32),
             pltpu.VMEM((more, channels), F32),
             pltpu.VMEM((more, channels), F32),
             pltpu.VMEM((more, channels), F32),
             pltpu.VMEM((own, channels), F32),
             pltpu.VMEM((own, channels), F32),
-            pltpu.VMEM((5, n, 2, channels), F32),
+            pltpu.VMEM((4, n, 2, channels), F32),
             pltpu.VMEM((m, 1, emb), F32),
-            pltpu.VMEM((m, 2, channels), F32),
+            pltpu.VMEM((m, n, 2, channels), F32),
+            pltpu.VMEM((n, GN_GROUPS, 4 * GN_GROUPS), F32),
             dma((11,)),
             dma((2, 2)),
             dma((2, 2)),
-            dma((5, n)),
-            dma((5, n)),
+            dma((4, n)),
+            dma((4, n)),
             dma((m,)),
             dma((m,)),
-            dma((m,)),
-            dma((m,)),
+            dma((n, m)),
+            dma((n, m)),
+            dma((n,)),
+            dma((n,)),
         ],
         compiler_params=pltpu.CompilerParams(
             collective_id=0, has_side_effects=True, vmem_limit_bytes=GRANT

time: 25.9 us -> 23 us (0.89)
  Pallas kernels: 23.8 us -> 20.9 us
    pallas_call x1, Pallas kernels: 22.9 us -> 20 us  [body(): pl.pallas_call(functools.partial(kernel, n, m), out_shape=(jax.ShapeDtype...]
where the time goes in v2:
time: 23 us; the launch traced here: 22.8 us
  Pallas kernels  20.9 us (91%)
  between operations  1.93 us (8%)
    pallas_call x1, Pallas kernels, body(): pl.pallas_call(functools.partial(kernel, n, m), out_shape=(jax.ShapeDtype...  20 us
    pallas_call x1, Pallas kernels, body(): pl.pallas_call(finish, out_shape=tuple((jax.ShapeDtypeStruct(r.shape, r.d...  0.92 us

profile of v2, /device:TPU:0, one launch (start us, length us, event | category | flops | bytes accessed | tf_op | source)
XLA Modules:
  0.0 22.8 jit_solution(16634824870058191150)
XLA Ops:
  1.9 20.0 %shard_map.156 = (bf16[1,4,64,256]{3,2,1,0:T(8,128)(2,1)S(1)}, bf16[1,4,64,256]{3,2,1,0:T(8,128)(2,1)S(1)}, f32[256,512]{1,0:T(8,128)S(1)}, f32[1,512]{1,0:T(1,128)S(1)}) custom-call(s32[1]{0:T(128)S(6)} %copy.17.steps_ref, s32[1]{0:T(128)S(6)} %copy.18.ids_ref, f32[1,256]{1,0:T(1,128)} %bitcast.6, f32[1,256]{1,0:T(1,128)} %bitcast.7, f32[1,256]{1,0:T(1,128)} %bitcast.8, ...), custom_call_target="tpu_custom_call" | custom-call | tf_op jit(solution)/shard_map/pallas_call | solution.py:546
  21.9 0.9 %shard_map.157 = (bf16[1,4,64,256]{3,2,1,0:T(8,128)(2,1)}, bf16[1,4,64,256]{3,2,1,0:T(8,128)(2,1)}, f32[256,512]{1,0:T(8,128)}, f32[1,512]{1,0:T(1,128)}) custom-call(bf16[1,4,64,256]{3,2,1,0:T(8,128)(2,1)S(1)} %get-tuple-element.12.refs_0_, bf16[1,4,64,256]{3,2,1,0:T(8,128)(2,1)S(1)} %get-tuple-element.13.refs_1_, ...), custom_call_target="tpu_custom_call" | custom-call | tf_op jit(solution)/shard_map/pallas_call | solution.py:613

commit v3 on v2

v3 whole, which is shorter than its diff:
```python
import functools
import math

import jax
import jax.numpy as jnp
from jax import lax
from jax.experimental import pallas as pl
from jax.experimental.pallas import tpu as pltpu
from jax.sharding import PartitionSpec as P

GN_GROUPS = 32
EPSILON = 1e-05
MESH = pl.DeviceIdType.MESH
F32 = jnp.float32
BF16 = jnp.bfloat16
GRANT = 24 << 20
REACH = 2
PARTS = 2
SPARE = 128
HIGHEST = lax.Precision.HIGHEST


def group_spread(values, width):
    count = values.shape[-1]
    lane = lax.broadcasted_iota(jnp.int32, values.shape, values.ndim - 1)
    step = 1
    while step < width:
        up = pltpu.roll(values, step, values.ndim - 1)
        down = pltpu.roll(values, count - step, values.ndim - 1)
        values = values + jnp.where((lane & step) != 0, up, down)
        step *= 2
    return values


def silu_slope(pre, sigma):
    return sigma * (1.0 + pre * (1.0 - sigma))


def column_sums(first, second):
    return jnp.concatenate(
        [jnp.sum(first, axis=0, keepdims=True), jnp.sum(second, axis=0, keepdims=True)], axis=0
    )


def kernel(
    n, m,
    steps_ref, ids_ref, gain_hbm, bias_hbm, tbias_hbm, abias_hbm,
    images_hbm, cot_hbm, first_hbm, second_hbm, tweight_hbm, table_hbm, aweight_hbm,
    branch, igrad, left_out, right_out, bgrad,
    images, cot, first, second, tweight, table, aweight,
    gain_ref, bias_ref, tbias_ref, abias_ref,
    wide_first, wide_cot, wide_second, wide_hidden,
    wide_scaled, wide_plain, tall, table_of,
    hidden, gact, nsecond, gpre, nfirst, slope,
    slots, acts, pairs, maps, spare,
    load_sem, halo_send, halo_recv, send_sem, slot_recv, act_recv, pair_recv, map_recv,
):
    me = lax.axis_index("tile")
    mine = lax.axis_index("image")
    rows, cols, channels = images_hbm.shape[1:]
    width = channels // GN_GROUPS
    cells = float(rows * cols * n * width)
    own = rows * cols
    above, below = me > 0, me < n - 1

    def load(source, target, k):
        return pltpu.make_async_copy(source, target, load_sem.at[k])

    loads = [
        load(images_hbm.at[0], images.at[pl.ds(REACH, rows)], 0),
        load(cot_hbm.at[0], cot.at[pl.ds(REACH, rows)], 1),
        load(tweight_hbm, tweight, 2),
        load(table_hbm, table, 3),
        load(aweight_hbm, aweight, 4),
        load(first_hbm, first, 5),
        load(second_hbm, second, 6),
        load(gain_hbm, gain_ref, 7),
        load(bias_hbm, bias_ref, 8),
        load(tbias_hbm, tbias_ref, 9),
        load(abias_hbm, abias_ref, 10),
    ]
    loads[0].start()
    barrier = pltpu.get_barrier_semaphore()
    for k in reversed(range(1, n)):
        pl.semaphore_signal(
            barrier, inc=1, device_id={"tile": lax.rem(me + k, n)}, device_id_type=MESH
        )
    for k in range(1, m):
        pl.semaphore_signal(
            barrier, inc=1, device_id={"image": lax.rem(mine + k, m)}, device_id_type=MESH
        )
    for k in (7, 8, 5, 2, 3, 4, 9, 10, 1, 6):
        loads[k].start()

    def remote(buffer, slot, receive, device):
        return pltpu.make_async_remote_copy(
            src_ref=buffer.at[slot],
            dst_ref=buffer.at[slot],
            send_sem=send_sem.at[0],
            recv_sem=receive,
            device_id=device,
            device_id_type=MESH,
        )

    def settle(lines, receive):
        while lines:
            part = min(lines, spare.shape[0])
            block = spare.at[pl.ds(0, part)]
            copy = pltpu.make_async_remote_copy(
                src_ref=block,
                dst_ref=block,
                send_sem=send_sem.at[0],
                recv_sem=send_sem.at[0] if receive is None else receive,
                device_id={"tile": lax.rem(me + 1, n)},
                device_id_type=MESH,
            )
            if receive is None:
                copy.wait_send()
            else:
                copy.wait_recv()
            lines -= part

    def tile_peer(k):
        return {"tile": lax.rem(me + k, n)}

    def share(stage, value):
        slots[stage, me] = value
        for k in range(1, n):
            remote(slots.at[stage], me, slot_recv.at[stage], tile_peer(k)).start()

    def total(stage):
        settle(2 * (n - 1), slot_recv.at[stage])
        summed = slots[stage, 0]
        for k in range(1, n):
            summed = summed + slots[stage, k]
        return summed

    HALOS = ((REACH, rows + REACH, rows + REACH - 1, REACH - 1, 1),
             (REACH + 1, rows + REACH + 1, rows + REACH - 2, REACH - 2, 1),
             (REACH, rows + REACH, rows, 0, REACH))

    def halo_copy(which, buffer, up):
        up_from, up_to, down_from, down_to, count = HALOS[which]
        source, target = (up_from, up_to) if up else (down_from, down_to)
        return pltpu.make_async_remote_copy(
            src_ref=buffer.at[pl.ds(source, count)],
            dst_ref=buffer.at[pl.ds(target, count)],
            send_sem=halo_send.at[which, int(up)],
            recv_sem=halo_recv.at[which, int(up)],
            device_id={"tile": me - 1 if up else me + 1},
            device_id_type=MESH,
        )

    def halo_start(which, buffer):
        _, low, _, high, count = HALOS[which]

        @pl.when(above)
        def _():
            halo_copy(which, buffer, True).start()

        @pl.when(below)
        def _():
            halo_copy(which, buffer, False).start()

        @pl.when(jnp.logical_not(above))
        def _():
            buffer[pl.ds(high, count)] = jnp.zeros((count, cols, channels), BF16)

        @pl.when(jnp.logical_not(below))
        def _():
            buffer[pl.ds(low, count)] = jnp.zeros((count, cols, channels), BF16)

    def halo_wait(which, buffer):
        @pl.when(below)
        def _():
            halo_copy(which, buffer, True).wait_recv()

        @pl.when(above)
        def _():
            halo_copy(which, buffer, False).wait_recv()

    column = lax.broadcasted_iota(jnp.int32, (cols, channels), 0)

    def widen(wide, row, values):
        before = jnp.where(column == 0, 0.0, pltpu.roll(values, 1, 0))
        after = jnp.where(column == cols - 1, 0.0, pltpu.roll(values, cols - 1, 0))
        at = pl.ds(row * cols, cols)
        wide[at, 0:channels] = before.astype(BF16)
        wide[at, channels : 2 * channels] = values.astype(BF16)
        wide[at, 2 * channels : 3 * channels] = after.astype(BF16)

    def conv(wide, starts, count, weight):
        summed = None
        for i in range(3):
            lines = [wide[pl.ds((start + i) * cols, count * cols), :] for start in starts]
            product = jnp.dot(
                lines[0] if len(lines) == 1 else jnp.concatenate(lines, axis=0),
                weight[i].reshape(3 * channels, channels),
                preferred_element_type=F32,
            )
            summed = product if summed is None else summed + product
        return summed

    def conv_back(wide, start, count, weight):
        summed = None
        for i in range(3):
            for j in range(3):
                product = lax.dot_general(
                    wide[pl.ds((start + i) * cols, count * cols), j * channels : (j + 1) * channels],
                    weight[2 - i, 2 - j],
                    (((1,), (1,)), ((), ())),
                    preferred_element_type=F32,
                )
                summed = product if summed is None else summed + product
        return summed

    def pieces(values):
        parts = []
        for _ in range(3):
            part = values.astype(BF16)
            parts.append(part)
            values = values - part.astype(F32)
        return parts

    def moments(summed):
        spread = group_spread(summed, width) / cells
        centre = spread[0:1]
        variance = jnp.maximum(spread[1:2] - centre * centre, 0.0)
        return centre, lax.rsqrt(variance + EPSILON)

    def add_up(parts):
        return functools.reduce(jnp.add, parts)

    loads[0].wait()
    sums = []
    for p in range(rows):
        line = images[REACH + p].astype(F32)
        sums.append(column_sums(line, line * line))
    sums = add_up(sums)
    pl.semaphore_wait(barrier, n - 1 + m - 1)
    share(0, sums)
    halo_start(0, images)
    halo_start(1, images)

    for k in (2, 3, 4, 7, 8, 9, 10):
        loads[k].wait()
    half = tweight.shape[0] // 2
    index = lax.broadcasted_iota(jnp.int32, (half, 1), 0).astype(F32)
    angles = steps_ref[0].astype(F32) * jnp.exp(-math.log(10000.0) * index / half)
    pre_time = (
        jnp.sum(jnp.cos(angles) * tweight[0:half].astype(F32), axis=0, keepdims=True)
        + jnp.sum(jnp.sin(angles) * tweight[half:].astype(F32), axis=0, keepdims=True)
        + tbias_ref[...]
    )
    entry = lax.broadcasted_iota(jnp.int32, table.shape, 0) == ids_ref[0]
    picked = jnp.sum(jnp.where(entry, table[...].astype(F32), 0.0), axis=0, keepdims=True)
    embedding = pre_time * jax.nn.sigmoid(pre_time) + picked
    activated = embedding * jax.nn.sigmoid(embedding)
    acts[mine] = activated
    for k in range(1, m):
        remote(acts, mine, act_recv.at[0], {"image": lax.rem(mine + k, m)}).start()
    partial = jnp.dot(
        jnp.broadcast_to(activated, (8, activated.shape[1])),
        aweight[...].astype(F32),
        precision=HIGHEST,
        preferred_element_type=F32,
    )[0:1]
    share(1, jnp.concatenate([partial[:, :channels], partial[:, channels:]], axis=0))

    loads[1].wait()
    halo_start(2, cot)
    for p in range(rows):
        widen(wide_cot, REACH + p, cot[REACH + p].astype(F32))

    loads[5].wait()
    halo_wait(0, images)
    gain, bias = gain_ref[...], bias_ref[...]
    centre, inverse_first = moments(total(0))
    stretch = 0.5 * inverse_first * gain
    offset = 0.5 * bias - centre * stretch

    def first_row(row, inside):
        lean = images[row].astype(F32) * stretch + offset
        value = lean * (1.0 + jnp.tanh(lean))
        if inside is not None:
            value = jnp.where(inside, value, 0.0)
        widen(wide_first, row, value)

    first_row(REACH - 1, above)
    for p in range(rows):
        first_row(REACH + p, None)
    first_row(rows + REACH, below)
    centre_rows = conv(wide_first, (1,), rows, first).astype(BF16).astype(F32)
    share(2, column_sums(centre_rows, centre_rows * centre_rows))
    hidden[pl.ds(cols, own)] = centre_rows

    halo_wait(1, images)
    first_row(0, above)
    first_row(rows + 2 * REACH - 1, below)
    outer = conv(wide_first, (0, rows + 1), 1, first).astype(BF16).astype(F32)
    hidden[pl.ds(0, cols)] = outer[0:cols]
    hidden[pl.ds((rows + 1) * cols, cols)] = outer[cols : 2 * cols]

    whole_rows, first_cells, last_cells = [[], []], [[], []], [[], []]
    for p in range(rows):
        at = pl.ds(p * cols, cols)
        line = images[REACH + p].astype(F32)
        lean = line * stretch + offset
        bend = jnp.tanh(lean)
        steep = (0.5 * gain) * ((1.0 + bend) * (1.0 + lean * (1.0 - bend)))
        line = (line - centre) * inverse_first
        nfirst[at] = line
        slope[at] = steep
        for part, lines in enumerate((steep, steep * line)):
            lines = lines.astype(BF16).astype(F32)
            gact[at if part == 0 else pl.ds((rows + p) * cols, cols)] = lines
            whole_rows[part].append(jnp.sum(lines, axis=0, keepdims=True))
            first_cells[part].append(lines[0:1])
            last_cells[part].append(lines[cols - 1 : cols])
    edges = []
    for part in range(2):
        tall[pl.ds(part * channels, channels), :] = gact[pl.ds(part * own, own)].T.astype(BF16)
        kept = [
            [a - b for a, b in zip(whole_rows[part], first_cells[part])],
            whole_rows[part],
            [a - b for a, b in zip(whole_rows[part], last_cells[part])],
        ]
        grid = []
        for i in range(3):
            for j in range(3):
                value = add_up(kept[j])
                if i == 0:
                    value = value - jnp.where(above, 0.0, kept[j][0])
                elif i == 2:
                    value = value - jnp.where(below, 0.0, kept[j][rows - 1])
                grid.append(value)
        edges.append(grid)
    for row in range(rows + 2):
        lines = hidden[pl.ds(row * cols, cols)]
        if row == 0:
            lines = jnp.where(above, lines, 0.0)
        elif row == rows + 1:
            lines = jnp.where(below, lines, 0.0)
        widen(wide_plain, row, lines)
    same = (
        lax.broadcasted_iota(jnp.int32, (GN_GROUPS, channels), 1) // width
        == lax.broadcasted_iota(jnp.int32, (GN_GROUPS, channels), 0)
    )
    products, constants = [None, None], None
    for i in range(3):
        for j in range(3):
            taps = first[2 - i, 2 - j]
            wide_taps = taps.astype(F32)
            near = wide_plain[pl.ds(i * cols, own), j * channels : (j + 1) * channels]
            for part in range(2):
                product = wide_taps * jnp.dot(
                    tall[pl.ds(part * channels, channels), :], near, preferred_element_type=F32
                )
                products[part] = product if i + j == 0 else products[part] + product
            spread_rows = [
                jnp.where(same, piece.astype(F32), 0.0)
                for part in range(2)
                for piece in pieces(edges[part][3 * i + j])
            ]
            product = jnp.dot(
                jnp.concatenate(spread_rows, axis=0).astype(BF16), taps, preferred_element_type=F32
            )
            constants = product if i + j == 0 else constants + product
    blocks = [
        jnp.sum(product.reshape(GN_GROUPS, width, channels), axis=1) for product in products
    ] + [
        add_up(
            [constants[(3 * part + q) * GN_GROUPS : (3 * part + q + 1) * GN_GROUPS] for q in range(3)]
        )
        for part in range(2)
    ]
    columns_of = [pieces(block) for block in blocks]
    lanes = 4 * GN_GROUPS
    gathered = None
    for quarter in range(4):
        row = lax.broadcasted_iota(jnp.int32, (channels, lanes), 0)
        lane = lax.broadcasted_iota(jnp.int32, (channels, lanes), 1)
        chosen = jnp.where(row // width + quarter * GN_GROUPS == lane, 1.0, 0.0).astype(BF16)
        product = jnp.dot(
            jnp.concatenate(columns_of[quarter], axis=0), chosen, preferred_element_type=F32
        )
        gathered = product if gathered is None else gathered + product
    maps[me] = add_up([gathered[q * GN_GROUPS : (q + 1) * GN_GROUPS] for q in range(3)])
    for k in range(1, n):
        remote(maps, me, map_recv.at[0], tile_peer(k)).start()

    halo_wait(2, cot)
    for row in (0, 1, rows + REACH, rows + REACH + 1):
        widen(wide_cot, row, cot[row].astype(F32))
    loads[6].wait()
    gact[pl.ds(0, (rows + 2) * cols)] = conv_back(wide_cot, 0, rows + 2, second)

    modulation = total(1)
    factor = 1.0 + (modulation[0:1] + abias_ref[:, :channels])
    shift = modulation[1:2] + abias_ref[:, channels:]
    centre, inverse_second = moments(total(2))

    def second_row(row):
        at = pl.ds(row * cols, cols)
        normed = (hidden[at] - centre) * inverse_second
        lean = normed * (0.5 * factor) + 0.5 * shift
        bend = jnp.tanh(lean)
        rise = 1.0 + bend
        back = gact[at] * (0.5 * rise * (1.0 + lean * (1.0 - bend)))
        nsecond[at] = normed
        gact[at] = lean * rise
        gpre[at] = back
        return column_sums(back * normed, back)

    pairs[mine, me] = add_up([second_row(1 + p) for p in range(rows)])
    others = [(k, step) for step in range(m) for k in range(n) if k or step]
    for k, step in others:
        remote(
            pairs.at[mine], me, pair_recv.at[min(step, 1)],
            {"tile": lax.rem(me + k, n), "image": lax.rem(mine + step, m)},
        ).start()

    scale = factor * inverse_second
    second_row(0)
    second_row(rows + 1)

    def masked(row, values):
        if row == 0:
            return jnp.where(above, values, 0.0)
        if row == rows + 1:
            return jnp.where(below, values, 0.0)
        return values

    for row in range(rows + 2):
        at = pl.ds(row * cols, cols)
        back = gpre[at] * scale
        gpre[at] = back
        widen(wide_scaled, row, masked(row, back))
    gradient = conv_back(wide_scaled, 0, rows, first)
    sums = []
    for p in range(rows):
        at = pl.ds(p * cols, cols)
        early = gradient[p * cols : (p + 1) * cols] * slope[at]
        sums.append(column_sums(early, early * nfirst[at]))
    share(3, add_up(sums))

    for row in range(rows + 2):
        widen(wide_second, row, masked(row, gact[pl.ds(row * cols, cols)]))
    branch[0] = conv(wide_second, (0,), rows, second).astype(BF16).reshape(rows, cols, channels)

    settle(maps.shape[1] * maps.shape[2] // channels * (n - 1), map_recv.at[0])
    summed = add_up([maps[k] for k in range(n)])
    spread_of = jnp.where(same, 1.0, 0.0)
    for q, piece in enumerate(pieces(summed)):
        table_of[pl.ds(q * lanes, lanes), :] = lax.dot_general(
            piece.astype(F32), spread_of, (((0,), (0,)), ((), ())), preferred_element_type=F32
        ).astype(BF16)

    settle((m - 1) * acts.shape[2] // channels, act_recv.at[0])
    extra = (-6 * m) % 16

    def stacked(parts):
        if extra:
            parts = parts + [jnp.zeros((extra, parts[0].shape[1]), F32)]
        return jnp.concatenate(parts, axis=0).astype(BF16)

    thirds = [[piece.astype(F32) for piece in pieces(acts[k])] for k in range(m)]
    left_out[...] = stacked([thirds[k][q] for q in (0, 0, 1, 0, 1, 2) for k in range(m)])

    settle(2 * (n - 1), pair_recv.at[0])

    def whole(image):
        return add_up([pairs[image, k] for k in range(n)])

    spread = group_spread(whole(mine) * factor, width) / cells
    paired_mean, plain_mean = inverse_second * spread[0:1], inverse_second * spread[1:2]
    for row in range(rows + 2):
        at = pl.ds(row * cols, cols)
        back = gpre[at] - plain_mean - nsecond[at] * paired_mean
        widen(wide_hidden, row, masked(row, back))

    tilt = paired_mean * inverse_second
    level = plain_mean - tilt * centre
    row = lax.broadcasted_iota(jnp.int32, (channels, lanes), 0)
    lane = lax.broadcasted_iota(jnp.int32, (channels, lanes), 1)
    chosen = jnp.where(lax.rem(lane, GN_GROUPS) * width == row, 1.0, 0.0).astype(BF16)
    short = [piece.astype(F32) for piece in pieces(level) + pieces(tilt)]
    short = jnp.concatenate(short + [jnp.zeros((2, channels), F32)], axis=0).astype(BF16)
    short = jnp.dot(short, chosen, preferred_element_type=F32)
    quarter = lax.broadcasted_iota(jnp.int32, (1, lanes), 1) // GN_GROUPS
    nothing = jnp.zeros((1, lanes), F32)
    left = []
    for part in range(2):
        mixed = [
            jnp.where(quarter == part, short[3 + q : 4 + q], jnp.where(quarter == part + 2, short[q : q + 1], 0.0))
            for q in range(3)
        ]
        left += [
            jnp.concatenate([mixed[q]] * (3 - q) + [nothing] * q, axis=1) for q in range(3)
        ]
    left = jnp.concatenate(left + [jnp.zeros((2, 3 * lanes), F32)], axis=0).astype(BF16)
    moved = jnp.dot(left, table_of[...], preferred_element_type=F32)
    moved = jnp.concatenate(
        [jnp.sum(moved[3 * part : 3 * part + 3], axis=0, keepdims=True) for part in range(2)], axis=0
    )

    gradient = conv_back(wide_hidden, 0, rows, first)

    settle(2 * n * (m - 1), pair_recv.at[1])
    sums = [whole(k) for k in range(m)]
    for part in range(2):
        lines = [value[part : part + 1] for value in sums]
        thirds = [[piece.astype(F32) for piece in pieces(line)] for line in lines]
        columns = slice(part * channels, (part + 1) * channels)
        right_out[:, columns] = stacked([thirds[k][q] for q in (0, 1, 0, 2, 1, 0) for k in range(m)])
        bgrad[:, columns] = add_up(lines)

    spread = (group_spread(total(3), width) - moved) / cells
    for p in range(rows):
        at = pl.ds(p * cols, cols)
        back = gradient[p * cols : (p + 1) * cols] * slope[at]
        result = inverse_first * (back - spread[0:1] - nfirst[at] * spread[1:2])
        igrad[0, p] = result.astype(BF16)

    lines = 2 * (4 * (n - 1) + len(others)) + (m - 1) * acts.shape[2] // channels
    lines += maps.shape[1] * maps.shape[2] // channels * (n - 1)
    settle(lines, None)
    for which, buffer in enumerate((images, images, cot)):

        @pl.when(above)
        def _():
            halo_copy(which, buffer, True).wait_send()

        @pl.when(below)
        def _():
            halo_copy(which, buffer, False).wait_send()


def finish(branch, igrad, left, right, bgrad, branch_out, igrad_out, wgrad_out, bgrad_out, wgrad, sem):
    copies = [
        pltpu.make_async_copy(source, target, sem.at[k])
        for k, (source, target) in enumerate(
            [(igrad, igrad_out), (branch, branch_out), (bgrad, bgrad_out)]
        )
    ]
    for copy in copies:
        copy.start()
    height = wgrad.shape[0] // PARTS
    for k in range(PARTS):
        at = pl.ds(k * height, height)
        wgrad[at] = lax.dot_general(
            left[:, k * height : (k + 1) * height], right[...],
            (((0,), (0,)), ((), ())), preferred_element_type=F32,
        )
        copy = pltpu.make_async_copy(wgrad.at[at], wgrad_out.at[at], sem.at[3 + k])
        copy.start()
        copies.append(copy)
    for copy in copies:
        copy.wait()


def body(
    n, m,
    images, cotangent, timesteps, class_ids, norm_gain, norm_bias, conv_first, conv_second,
    time_weight, time_bias, class_table, adaptive_weight, adaptive_bias,
):
    count, rows, cols, channels = images.shape
    assert count == 1 and rows >= REACH
    emb = time_weight.shape[1]
    vmem = pl.BlockSpec(memory_space=pltpu.VMEM)
    anywhere = pl.BlockSpec(memory_space=pl.ANY)
    padded = rows + 2 * REACH
    stack = 6 * m + (-6 * m) % 16
    own, more, most = rows * cols, (rows + 2) * cols, padded * cols
    dma = pltpu.SemaphoreType.DMA
    results = pl.pallas_call(
        functools.partial(kernel, n, m),
        out_shape=(
            jax.ShapeDtypeStruct(images.shape, BF16),
            jax.ShapeDtypeStruct(images.shape, BF16),
            jax.ShapeDtypeStruct((stack, emb), BF16),
            jax.ShapeDtypeStruct((stack, 2 * channels), BF16),
            jax.ShapeDtypeStruct((1, 2 * channels), F32),
        ),
        in_specs=[pl.BlockSpec(memory_space=pltpu.SMEM)] * 2
        + [pl.BlockSpec(memory_space=pltpu.HBM)] * 11,
        out_specs=(vmem,) * 5,
        scratch_shapes=[
            pltpu.VMEM((padded, cols, channels), BF16),
            pltpu.VMEM((padded, cols, channels), BF16),
            pltpu.VMEM(conv_first.shape, BF16),
            pltpu.VMEM(conv_second.shape, BF16),
            pltpu.VMEM(time_weight.shape, BF16),
            pltpu.VMEM(class_table.shape, BF16),
            pltpu.VMEM(adaptive_weight.shape, BF16),
            pltpu.VMEM((1, channels), F32),
            pltpu.VMEM((1, channels), F32),
            pltpu.VMEM((1, emb), F32),
            pltpu.VMEM((1, 2 * channels), F32),
            pltpu.VMEM((most, 3 * channels), BF16),
            pltpu.VMEM((most, 3 * channels), BF16),
            pltpu.VMEM((more, 3 * channels), BF16),
            pltpu.VMEM((more, 3 * channels), BF16),
            pltpu.VMEM((more, 3 * channels), BF16),
            pltpu.VMEM((more, 3 * channels), BF16),
            pltpu.VMEM((2 * channels, own), BF16),
            pltpu.VMEM((12 * GN_GROUPS, channels), BF16),
            pltpu.VMEM((more, channels), F32),
            pltpu.VMEM((max(more, 2 * own), channels), F32),
            pltpu.VMEM((more, channels), F32),
            pltpu.VMEM((more, channels), F32),
            pltpu.VMEM((own, channels), F32),
            pltpu.VMEM((own, channels), F32),
            pltpu.VMEM((4, n, 2, channels), F32),
            pltpu.VMEM((m, 1, emb), F32),
            pltpu.VMEM((m, n, 2, channels), F32),
            pltpu.VMEM((n, GN_GROUPS, 4 * GN_GROUPS), F32),
            pltpu.VMEM((SPARE, 1, channels), F32),
            dma((11,)),
            dma((3, 2)),
            dma((3, 2)),
            dma((1,)),
            dma((4,)),
            dma((1,)),
            dma((2,)),
            dma((1,)),
        ],
        compiler_params=pltpu.CompilerParams(
            collective_id=0, has_side_effects=True, vmem_limit_bytes=GRANT
        ),
    )(
        timesteps, class_ids,
        *(
            pltpu.with_memory_space_constraint(operand, pltpu.HBM)
            for operand in (
                norm_gain[None], norm_bias[None], time_bias[None],
                adaptive_bias[None], images, cotangent, conv_first, conv_second, time_weight,
                class_table, adaptive_weight,
            )
        )
    )
    branch, igrad, wgrad, bgrad = pl.pallas_call(
        finish,
        out_shape=(
            jax.ShapeDtypeStruct(images.shape, BF16),
            jax.ShapeDtypeStruct(images.shape, BF16),
            jax.ShapeDtypeStruct((emb, 2 * channels), F32),
            jax.ShapeDtypeStruct((1, 2 * channels), F32),
        ),
        in_specs=[anywhere] * 2 + [vmem] * 2 + [anywhere],
        out_specs=(anywhere,) * 4,
        scratch_shapes=[pltpu.VMEM((emb, 2 * channels), F32), dma((3 + PARTS,))],
        compiler_params=pltpu.CompilerParams(vmem_limit_bytes=GRANT),
    )(*results)
    return branch, igrad, wgrad, bgrad[0]


def solution(mesh):
    return jax.shard_map(
        functools.partial(body, mesh.shape["tile"], mesh.shape["image"]),
        mesh=mesh,
        in_specs=(
            P(("groups", "image"), "tile", None, None),
            P(("groups", "image"), "tile", None, None),
            P(("groups", "image")),
            P(("groups", "image")),
            P(),
            P(),
            P(),
            P(),
            P(None, "tile"),
            P("tile"),
            P(None, "tile"),
            P("tile", None),
            P(),
        ),
        out_specs=(
            P(("groups", "image"), "tile", None, None),
            P(("groups", "image"), "tile", None, None),
            P(("groups", "tile"), None),
            P("groups"),
        ),
        check_vma=False,
    )
```

time: 23 us -> 21.8 us (0.948)
  Pallas kernels: 20.9 us -> 19.7 us
    pallas_call x1, Pallas kernels: 20 us -> 18.6 us  [body(): pl.pallas_call(functools.partial(kernel, n, m), out_shape=(jax.ShapeDtype...]
where the time goes in v3:
time: 21.8 us; the launch traced here: 21.6 us
  Pallas kernels  19.7 us (90%)
  between operations  1.93 us (9%)
    pallas_call x1, Pallas kernels, body(): pl.pallas_call(functools.partial(kernel, n, m), out_shape=(jax.ShapeDtype...  18.6 us
    pallas_call x1, Pallas kernels, body(): pl.pallas_call(finish, out_shape=(jax.ShapeDtypeStruct(images.shape, BF16...  1.04 us

profile of v3, /device:TPU:0, one launch (start us, length us, event | category | flops | bytes accessed | tf_op | source)
XLA Modules:
  0.0 21.6 jit_solution(16257285553751535681)
XLA Ops:
  1.9 18.6 %shard_map.156 = (bf16[1,4,64,256]{3,2,1,0:T(8,128)(2,1)S(1)}, bf16[1,4,64,256]{3,2,1,0:T(8,128)(2,1)S(1)}, bf16[32,256]{1,0:T(8,128)(2,1)S(1)}, bf16[32,512]{1,0:T(8,128)(2,1)S(1)}, f32[1,512]{1,0:T(1,128)S(1)}) custom-call(s32[1]{0:T(128)S(6)} %copy.17.steps_ref, s32[1]{0:T(128)S(6)} %copy.18.ids_ref, f32[1,256]{1,0:T(1,128)} %bitcast.6, ...), custom_call_target="tpu_custom_call" | custom-call | tf_op jit(solution)/shard_map/pallas_call | solution.py:576
  20.6 1.0 %shard_map.157 = (bf16[1,4,64,256]{3,2,1,0:T(8,128)(2,1)}, bf16[1,4,64,256]{3,2,1,0:T(8,128)(2,1)}, f32[256,512]{1,0:T(8,128)}, f32[1,512]{1,0:T(1,128)}) custom-call(bf16[1,4,64,256]{3,2,1,0:T(8,128)(2,1)S(1)} %get-tuple-element.13.branch, bf16[1,4,64,256]{3,2,1,0:T(8,128)(2,1)S(1)} %get-tuple-element.14.igrad, bf16[32,256]{1,0:T(8,128)(2,1)S(1)} %get-tuple-element.15.left, ...), custom_call_target="tpu_custom_call" | custom-call | tf_op jit(solution)/shard_map/pallas_call | solution.py:642

commit v4 on v3

--- a/solution.py
+++ b/solution.py
@@ -49,8 +49,7 @@
     branch, igrad, left_out, right_out, bgrad,
     images, cot, first, second, tweight, table, aweight,
     gain_ref, bias_ref, tbias_ref, abias_ref,
-    wide_first, wide_cot, wide_second, wide_hidden,
-    wide_scaled, wide_plain, tall, table_of,
+    near_first, near_second, near_hidden, near_scaled, wide_plain, tall, table_of,
     hidden, gact, nsecond, gpre, nfirst, slope,
     slots, acts, pairs, maps, spare,
     load_sem, halo_send, halo_recv, send_sem, slot_recv, act_recv, pair_recv, map_recv,
@@ -189,30 +188,45 @@
         wide[at, channels : 2 * channels] = values.astype(BF16)
         wide[at, 2 * channels : 3 * channels] = after.astype(BF16)
 
-    def conv(wide, starts, count, weight):
-        summed = None
-        for i in range(3):
-            lines = [wide[pl.ds((start + i) * cols, count * cols), :] for start in starts]
-            product = jnp.dot(
-                lines[0] if len(lines) == 1 else jnp.concatenate(lines, axis=0),
-                weight[i].reshape(3 * channels, channels),
-                preferred_element_type=F32,
-            )
-            summed = product if summed is None else summed + product
-        return summed
-
-    def conv_back(wide, start, count, weight):
-        summed = None
-        for i in range(3):
-            for j in range(3):
+    edge = jnp.zeros((1, channels), F32)
+
+    def shifted(parts, count):
+        lines = []
+        for p in range(count):
+            before, at, after = [part[p * cols : (p + 1) * cols] for part in parts]
+            before = jnp.concatenate([edge, before[: cols - 1]], axis=0)
+            after = jnp.concatenate([after[1:], edge], axis=0)
+            lines.append(at + (before + after))
+        return lines
+
+    def conv(near, starts, count, weight):
+        parts = [None] * 3
+        for j in (0, 2, 1):
+            for i in range(3):
+                lines = [near[pl.ds((start + i) * cols, count * cols), :] for start in starts]
+                product = jnp.dot(
+                    lines[0] if len(lines) == 1 else jnp.concatenate(lines, axis=0),
+                    weight[i, j],
+                    preferred_element_type=F32,
+                )
+                parts[j] = product if i == 0 else parts[j] + product
+        return shifted(parts, count * len(starts))
+
+    def conv_back(lines_of, count, weight):
+        parts = [None] * 3
+        for j in (0, 2, 1):
+            for i in range(3):
                 product = lax.dot_general(
-                    wide[pl.ds((start + i) * cols, count * cols), j * channels : (j + 1) * channels],
+                    lines_of(i),
                     weight[2 - i, 2 - j],
                     (((1,), (1,)), ((), ())),
                     preferred_element_type=F32,
                 )
-                summed = product if summed is None else summed + product
-        return summed
+                parts[j] = product if i == 0 else parts[j] + product
+        return shifted(parts, count)
+
+    def window(near, count):
+        return lambda i: near[pl.ds(i * cols, count * cols), :]
 
     def pieces(values):
         parts = []
@@ -231,12 +245,19 @@
     def add_up(parts):
         return functools.reduce(jnp.add, parts)
 
+    def gathered_sums(lines):
+        folded = [
+            add_up([jnp.sum(line[q].reshape(cols // 8, 8, channels), axis=0) for line in lines])
+            for q in range(2)
+        ]
+        return column_sums(*folded)
+
     loads[0].wait()
     sums = []
     for p in range(rows):
         line = images[REACH + p].astype(F32)
-        sums.append(column_sums(line, line * line))
-    sums = add_up(sums)
+        sums.append((line, line * line))
+    sums = gathered_sums(sums)
     pl.semaphore_wait(barrier, n - 1 + m - 1)
     share(0, sums)
     halo_start(0, images)
@@ -269,8 +290,6 @@
 
     loads[1].wait()
     halo_start(2, cot)
-    for p in range(rows):
-        widen(wide_cot, REACH + p, cot[REACH + p].astype(F32))
 
     loads[5].wait()
     halo_wait(0, images)
@@ -284,22 +303,24 @@
         value = lean * (1.0 + jnp.tanh(lean))
         if inside is not None:
             value = jnp.where(inside, value, 0.0)
-        widen(wide_first, row, value)
+        near_first[pl.ds(row * cols, cols)] = value.astype(BF16)
 
     first_row(REACH - 1, above)
     for p in range(rows):
         first_row(REACH + p, None)
     first_row(rows + REACH, below)
-    centre_rows = conv(wide_first, (1,), rows, first).astype(BF16).astype(F32)
-    share(2, column_sums(centre_rows, centre_rows * centre_rows))
-    hidden[pl.ds(cols, own)] = centre_rows
+    centre_rows = [
+        line.astype(BF16).astype(F32) for line in conv(near_first, (1,), rows, first)
+    ]
+    share(2, gathered_sums([(line, line * line) for line in centre_rows]))
+    for p, line in enumerate(centre_rows):
+        hidden[pl.ds((1 + p) * cols, cols)] = line
 
     halo_wait(1, images)
     first_row(0, above)
     first_row(rows + 2 * REACH - 1, below)
-    outer = conv(wide_first, (0, rows + 1), 1, first).astype(BF16).astype(F32)
-    hidden[pl.ds(0, cols)] = outer[0:cols]
-    hidden[pl.ds((rows + 1) * cols, cols)] = outer[cols : 2 * cols]
+    for row, line in zip((0, rows + 1), conv(near_first, (0, rows + 1), 1, first)):
+        hidden[pl.ds(row * cols, cols)] = line.astype(BF16).astype(F32)
 
     whole_rows, first_cells, last_cells = [[], []], [[], []], [[], []]
     for p in range(rows):
@@ -390,10 +411,10 @@
         remote(maps, me, map_recv.at[0], tile_peer(k)).start()
 
     halo_wait(2, cot)
-    for row in (0, 1, rows + REACH, rows + REACH + 1):
-        widen(wide_cot, row, cot[row].astype(F32))
     loads[6].wait()
-    gact[pl.ds(0, (rows + 2) * cols)] = conv_back(wide_cot, 0, rows + 2, second)
+    spans = lambda i: cot[pl.ds(i, rows + 2)].reshape((rows + 2) * cols, channels)
+    for row, line in enumerate(conv_back(spans, rows + 2, second)):
+        gact[pl.ds(row * cols, cols)] = line
 
     modulation = total(1)
     factor = 1.0 + (modulation[0:1] + abias_ref[:, :channels])
@@ -410,9 +431,9 @@
         nsecond[at] = normed
         gact[at] = lean * rise
         gpre[at] = back
-        return column_sums(back * normed, back)
-
-    pairs[mine, me] = add_up([second_row(1 + p) for p in range(rows)])
+        return back * normed, back
+
+    pairs[mine, me] = gathered_sums([second_row(1 + p) for p in range(rows)])
     others = [(k, step) for step in range(m) for k in range(n) if k or step]
     for k, step in others:
         remote(
@@ -435,18 +456,20 @@
         at = pl.ds(row * cols, cols)
         back = gpre[at] * scale
         gpre[at] = back
-        widen(wide_scaled, row, masked(row, back))
-    gradient = conv_back(wide_scaled, 0, rows, first)
+        near_scaled[at] = masked(row, back).astype(BF16)
+    gradient = conv_back(window(near_scaled, rows), rows, first)
     sums = []
     for p in range(rows):
         at = pl.ds(p * cols, cols)
-        early = gradient[p * cols : (p + 1) * cols] * slope[at]
-        sums.append(column_sums(early, early * nfirst[at]))
-    share(3, add_up(sums))
+        early = gradient[p] * slope[at]
+        sums.append((early, early * nfirst[at]))
+    share(3, gathered_sums(sums))
 
     for row in range(rows + 2):
-        widen(wide_second, row, masked(row, gact[pl.ds(row * cols, cols)]))
-    branch[0] = conv(wide_second, (0,), rows, second).astype(BF16).reshape(rows, cols, channels)
+        at = pl.ds(row * cols, cols)
+        near_second[at] = masked(row, gact[at]).astype(BF16)
+    for p, line in enumerate(conv(near_second, (0,), rows, second)):
+        branch[0, p] = line.astype(BF16)
 
     settle(maps.shape[1] * maps.shape[2] // channels * (n - 1), map_recv.at[0])
     summed = add_up([maps[k] for k in range(n)])
@@ -477,7 +500,7 @@
     for row in range(rows + 2):
         at = pl.ds(row * cols, cols)
         back = gpre[at] - plain_mean - nsecond[at] * paired_mean
-        widen(wide_hidden, row, masked(row, back))
+        near_hidden[at] = masked(row, back).astype(BF16)
 
     tilt = paired_mean * inverse_second
     level = plain_mean - tilt * centre
@@ -504,7 +527,14 @@
         [jnp.sum(moved[3 * part : 3 * part + 3], axis=0, keepdims=True) for part in range(2)], axis=0
     )
 
-    gradient = conv_back(wide_hidden, 0, rows, first)
+    gradient = conv_back(window(near_hidden, rows), rows, first)
+
+    spread = (group_spread(total(3), width) - moved) / cells
+    for p in range(rows):
+        at = pl.ds(p * cols, cols)
+        back = gradient[p] * slope[at]
+        result = inverse_first * (back - spread[0:1] - nfirst[at] * spread[1:2])
+        igrad[0, p] = result.astype(BF16)
 
     settle(2 * n * (m - 1), pair_recv.at[1])
     sums = [whole(k) for k in range(m)]
@@ -514,13 +544,6 @@
         columns = slice(part * channels, (part + 1) * channels)
         right_out[:, columns] = stacked([thirds[k][q] for q in (0, 1, 0, 2, 1, 0) for k in range(m)])
         bgrad[:, columns] = add_up(lines)
-
-    spread = (group_spread(total(3), width) - moved) / cells
-    for p in range(rows):
-        at = pl.ds(p * cols, cols)
-        back = gradient[p * cols : (p + 1) * cols] * slope[at]
-        result = inverse_first * (back - spread[0:1] - nfirst[at] * spread[1:2])
-        igrad[0, p] = result.astype(BF16)
 
     lines = 2 * (4 * (n - 1) + len(others)) + (m - 1) * acts.shape[2] // channels
     lines += maps.shape[1] * maps.shape[2] // channels * (n - 1)
@@ -597,11 +620,10 @@
             pltpu.VMEM((1, channels), F32),
             pltpu.VMEM((1, emb), F32),
             pltpu.VMEM((1, 2 * channels), F32),
-            pltpu.VMEM((most, 3 * channels), BF16),
-            pltpu.VMEM((most, 3 * channels), BF16),
-            pltpu.VMEM((more, 3 * channels), BF16),
-            pltpu.VMEM((more, 3 * channels), BF16),
-            pltpu.VMEM((more, 3 * channels), BF16),
+            pltpu.VMEM((most, channels), BF16),
+            pltpu.VMEM((more, channels), BF16),
+            pltpu.VMEM((more, channels), BF16),
+            pltpu.VMEM((more, channels), BF16),
             pltpu.VMEM((more, 3 * channels), BF16),
             pltpu.VMEM((2 * channels, own), BF16),
             pltpu.VMEM((12 * GN_GROUPS, channels), BF16),

time: 21.8 us -> 21.2 us (0.972)
  Pallas kernels: 19.7 us -> 19.1 us
    pallas_call x1, Pallas kernels: 18.6 us -> 18.1 us  [body(): pl.pallas_call(functools.partial(kernel, n, m), out_shape=(jax.ShapeDtype...]
where the time goes in v4:
time: 21.2 us; the launch traced here: 21 us
  Pallas kernels  19.1 us (90%)
  between operations  1.93 us (9%)
    pallas_call x1, Pallas kernels, body(): pl.pallas_call(functools.partial(kernel, n, m), out_shape=(jax.ShapeDtype...  18.1 us
    pallas_call x1, Pallas kernels, body(): pl.pallas_call(finish, out_shape=(jax.ShapeDtypeStruct(images.shape, BF16...  1.04 us

profile of v4, /device:TPU:0, one launch (start us, length us, event | category | flops | bytes accessed | tf_op | source)
XLA Modules:
  0.0 21.0 jit_solution(8621738816206385759)
XLA Ops:
  1.9 18.1 %shard_map.156 = (bf16[1,4,64,256]{3,2,1,0:T(8,128)(2,1)S(1)}, bf16[1,4,64,256]{3,2,1,0:T(8,128)(2,1)S(1)}, bf16[32,256]{1,0:T(8,128)(2,1)S(1)}, bf16[32,512]{1,0:T(8,128)(2,1)S(1)}, f32[1,512]{1,0:T(1,128)S(1)}) custom-call(s32[1]{0:T(128)S(6)} %copy.17.steps_ref, s32[1]{0:T(128)S(6)} %copy.18.ids_ref, f32[1,256]{1,0:T(1,128)} %bitcast.6, ...), custom_call_target="tpu_custom_call" | custom-call | tf_op jit(solution)/shard_map/pallas_call | solution.py:599
  20.0 1.0 %shard_map.157 = (bf16[1,4,64,256]{3,2,1,0:T(8,128)(2,1)}, bf16[1,4,64,256]{3,2,1,0:T(8,128)(2,1)}, f32[256,512]{1,0:T(8,128)}, f32[1,512]{1,0:T(1,128)}) custom-call(bf16[1,4,64,256]{3,2,1,0:T(8,128)(2,1)S(1)} %get-tuple-element.13.branch, bf16[1,4,64,256]{3,2,1,0:T(8,128)(2,1)S(1)} %get-tuple-element.14.igrad, bf16[32,256]{1,0:T(8,128)(2,1)S(1)} %get-tuple-element.15.left, ...), custom_call_target="tpu_custom_call" | custom-call | tf_op jit(solution)/shard_map/pallas_call | solution.py:664

commit v5 on v4

--- a/solution.py
+++ b/solution.py
@@ -47,7 +47,7 @@
     steps_ref, ids_ref, gain_hbm, bias_hbm, tbias_hbm, abias_hbm,
     images_hbm, cot_hbm, first_hbm, second_hbm, tweight_hbm, table_hbm, aweight_hbm,
     branch, igrad, left_out, right_out, bgrad,
-    images, cot, first, second, tweight, table, aweight,
+    images, cot, first, second, first_back, second_back, tweight, table, aweight,
     gain_ref, bias_ref, tbias_ref, abias_ref,
     near_first, near_second, near_hidden, near_scaled, wide_plain, tall, table_of,
     hidden, gact, nsecond, gpre, nfirst, slope,
@@ -216,17 +216,16 @@
         parts = [None] * 3
         for j in (0, 2, 1):
             for i in range(3):
-                product = lax.dot_general(
-                    lines_of(i),
-                    weight[2 - i, 2 - j],
-                    (((1,), (1,)), ((), ())),
-                    preferred_element_type=F32,
+                product = jnp.dot(
+                    lines_of(i), weight[2 - i, 2 - j], preferred_element_type=F32
                 )
                 parts[j] = product if i == 0 else parts[j] + product
         return shifted(parts, count)
 
-    def window(near, count):
-        return lambda i: near[pl.ds(i * cols, count * cols), :]
+    def window(near, start, count):
+        return lambda i: near[pl.ds((start + i) * cols, count * cols), :]
+
+    halves = [(0, rows // 2), (rows // 2, rows - rows // 2)]
 
     def pieces(values):
         parts = []
@@ -291,7 +290,11 @@
     loads[1].wait()
     halo_start(2, cot)
 
-    loads[5].wait()
+    for k, weight, turned in ((5, first, first_back), (6, second, second_back)):
+        loads[k].wait()
+        for i in range(3):
+            for j in range(3):
+                turned[i, j] = weight[i, j].T
     halo_wait(0, images)
     gain, bias = gain_ref[...], bias_ref[...]
     centre, inverse_first = moments(total(0))
@@ -305,13 +308,16 @@
             value = jnp.where(inside, value, 0.0)
         near_first[pl.ds(row * cols, cols)] = value.astype(BF16)
 
-    first_row(REACH - 1, above)
-    for p in range(rows):
-        first_row(REACH + p, None)
-    first_row(rows + REACH, below)
-    centre_rows = [
-        line.astype(BF16).astype(F32) for line in conv(near_first, (1,), rows, first)
-    ]
+    centre_rows, done = [], 0
+    for start, count in halves:
+        while done < start + count + 2:
+            row = REACH - 1 + done
+            first_row(row, above if done == 0 else below if done == rows + 1 else None)
+            done += 1
+        centre_rows += [
+            line.astype(BF16).astype(F32)
+            for line in conv(near_first, (1 + start,), count, first)
+        ]
     share(2, gathered_sums([(line, line * line) for line in centre_rows]))
     for p, line in enumerate(centre_rows):
         hidden[pl.ds((1 + p) * cols, cols)] = line
@@ -411,10 +417,11 @@
         remote(maps, me, map_recv.at[0], tile_peer(k)).start()
 
     halo_wait(2, cot)
-    loads[6].wait()
-    spans = lambda i: cot[pl.ds(i, rows + 2)].reshape((rows + 2) * cols, channels)
-    for row, line in enumerate(conv_back(spans, rows + 2, second)):
-        gact[pl.ds(row * cols, cols)] = line
+    count = (rows + 2) // 2
+    for start in (0, rows + 2 - count):
+        spans = lambda i: cot[pl.ds(start + i, count)].reshape(count * cols, channels)
+        for p, line in enumerate(conv_back(spans, count, second_back)):
+            gact[pl.ds((start + p) * cols, cols)] = line
 
     modulation = total(1)
     factor = 1.0 + (modulation[0:1] + abias_ref[:, :channels])
@@ -452,24 +459,26 @@
             return jnp.where(below, values, 0.0)
         return values
 
-    for row in range(rows + 2):
-        at = pl.ds(row * cols, cols)
-        back = gpre[at] * scale
-        gpre[at] = back
-        near_scaled[at] = masked(row, back).astype(BF16)
-    gradient = conv_back(window(near_scaled, rows), rows, first)
-    sums = []
-    for p in range(rows):
-        at = pl.ds(p * cols, cols)
-        early = gradient[p] * slope[at]
-        sums.append((early, early * nfirst[at]))
+    sums, done = [], 0
+    for start, count in halves:
+        while done < start + count + 2:
+            at = pl.ds(done * cols, cols)
+            back = gpre[at] * scale
+            gpre[at] = back
+            near_scaled[at] = masked(done, back).astype(BF16)
+            done += 1
+        for p, line in enumerate(conv_back(window(near_scaled, start, count), count, first_back)):
+            at = pl.ds((start + p) * cols, cols)
+            early = line * slope[at]
+            sums.append((early, early * nfirst[at]))
     share(3, gathered_sums(sums))
 
     for row in range(rows + 2):
         at = pl.ds(row * cols, cols)
         near_second[at] = masked(row, gact[at]).astype(BF16)
-    for p, line in enumerate(conv(near_second, (0,), rows, second)):
-        branch[0, p] = line.astype(BF16)
+    for start, count in halves:
+        for p, line in enumerate(conv(near_second, (start,), count, second)):
+            branch[0, start + p] = line.astype(BF16)
 
     settle(maps.shape[1] * maps.shape[2] // channels * (n - 1), map_recv.at[0])
     summed = add_up([maps[k] for k in range(n)])
@@ -497,10 +506,14 @@
 
     spread = group_spread(whole(mine) * factor, width) / cells
     paired_mean, plain_mean = inverse_second * spread[0:1], inverse_second * spread[1:2]
-    for row in range(rows + 2):
-        at = pl.ds(row * cols, cols)
-        back = gpre[at] - plain_mean - nsecond[at] * paired_mean
-        near_hidden[at] = masked(row, back).astype(BF16)
+    gradient, done = [], 0
+    for start, count in halves:
+        while done < start + count + 2:
+            at = pl.ds(done * cols, cols)
+            back = gpre[at] - plain_mean - nsecond[at] * paired_mean
+            near_hidden[at] = masked(done, back).astype(BF16)
+            done += 1
+        gradient += conv_back(window(near_hidden, start, count), count, first_back)
 
     tilt = paired_mean * inverse_second
     level = plain_mean - tilt * centre
@@ -526,8 +539,6 @@
     moved = jnp.concatenate(
         [jnp.sum(moved[3 * part : 3 * part + 3], axis=0, keepdims=True) for part in range(2)], axis=0
     )
-
-    gradient = conv_back(window(near_hidden, rows), rows, first)
 
     spread = (group_spread(total(3), width) - moved) / cells
     for p in range(rows):
@@ -611,6 +622,8 @@
         scratch_shapes=[
             pltpu.VMEM((padded, cols, channels), BF16),
             pltpu.VMEM((padded, cols, channels), BF16),
+            pltpu.VMEM(conv_first.shape, BF16),
+            pltpu.VMEM(conv_second.shape, BF16),
             pltpu.VMEM(conv_first.shape, BF16),
             pltpu.VMEM(conv_second.shape, BF16),
             pltpu.VMEM(time_weight.shape, BF16),

time: 21.2 us -> 21 us (level)
  no operation moved by 1% of the time
where the time goes in v5:
time: 21 us; the launch traced here: 20.9 us
  Pallas kernels  18.9 us (90%)
  between operations  1.93 us (9%)
    pallas_call x1, Pallas kernels, body(): pl.pallas_call(functools.partial(kernel, n, m), out_shape=(jax.ShapeDtype...  17.9 us
    pallas_call x1, Pallas kernels, body(): pl.pallas_call(finish, out_shape=(jax.ShapeDtypeStruct(images.shape, BF16...  1.04 us

profile of v5, /device:TPU:0, one launch (start us, length us, event | category | flops | bytes accessed | tf_op | source)
XLA Modules:
  0.0 20.9 jit_solution(5015007747591954292)
XLA Ops:
  1.9 17.9 %shard_map.156 = (bf16[1,4,64,256]{3,2,1,0:T(8,128)(2,1)S(1)}, bf16[1,4,64,256]{3,2,1,0:T(8,128)(2,1)S(1)}, bf16[32,256]{1,0:T(8,128)(2,1)S(1)}, bf16[32,512]{1,0:T(8,128)(2,1)S(1)}, f32[1,512]{1,0:T(1,128)S(1)}) custom-call(s32[1]{0:T(128)S(6)} %copy.17.steps_ref, s32[1]{0:T(128)S(6)} %copy.18.ids_ref, f32[1,256]{1,0:T(1,128)} %bitcast.6, ...), custom_call_target="tpu_custom_call" | custom-call | tf_op jit(solution)/shard_map/pallas_call | solution.py:610
  19.8 1.0 %shard_map.157 = (bf16[1,4,64,256]{3,2,1,0:T(8,128)(2,1)}, bf16[1,4,64,256]{3,2,1,0:T(8,128)(2,1)}, f32[256,512]{1,0:T(8,128)}, f32[1,512]{1,0:T(1,128)}) custom-call(bf16[1,4,64,256]{3,2,1,0:T(8,128)(2,1)S(1)} %get-tuple-element.13.branch, bf16[1,4,64,256]{3,2,1,0:T(8,128)(2,1)S(1)} %get-tuple-element.14.igrad, bf16[32,256]{1,0:T(8,128)(2,1)S(1)} %get-tuple-element.15.left, ...), custom_call_target="tpu_custom_call" | custom-call | tf_op jit(solution)/shard_map/pallas_call | solution.py:677

commit v6 on v5

--- a/solution.py
+++ b/solution.py
@@ -22,14 +22,16 @@
 
 def group_spread(values, width):
     count = values.shape[-1]
-    lane = lax.broadcasted_iota(jnp.int32, values.shape, values.ndim - 1)
-    step = 1
-    while step < width:
-        up = pltpu.roll(values, step, values.ndim - 1)
-        down = pltpu.roll(values, count - step, values.ndim - 1)
-        values = values + jnp.where((lane & step) != 0, up, down)
-        step *= 2
-    return values
+    place = lax.broadcasted_iota(jnp.int32, values.shape, values.ndim - 1) % width
+    terms = [values]
+    for step in range(1, width):
+        ahead = pltpu.roll(values, count - step, values.ndim - 1)
+        wrapped = pltpu.roll(values, width - step, values.ndim - 1)
+        terms.append(jnp.where(place + step < width, ahead, wrapped))
+    while len(terms) > 1:
+        pairs = [left + right for left, right in zip(terms[::2], terms[1::2])]
+        terms = pairs + terms[2 * len(pairs) :]
+    return terms[0]
 
 
 def silu_slope(pre, sigma):
@@ -236,7 +238,7 @@
         return parts
 
     def moments(summed):
-        spread = group_spread(summed, width) / cells
+        spread = summed / cells
         centre = spread[0:1]
         variance = jnp.maximum(spread[1:2] - centre * centre, 0.0)
         return centre, lax.rsqrt(variance + EPSILON)
@@ -256,7 +258,7 @@
     for p in range(rows):
         line = images[REACH + p].astype(F32)
         sums.append((line, line * line))
-    sums = gathered_sums(sums)
+    sums = group_spread(gathered_sums(sums), width)
     pl.semaphore_wait(barrier, n - 1 + m - 1)
     share(0, sums)
     halo_start(0, images)
@@ -426,7 +428,7 @@
     modulation = total(1)
     factor = 1.0 + (modulation[0:1] + abias_ref[:, :channels])
     shift = modulation[1:2] + abias_ref[:, channels:]
-    centre, inverse_second = moments(total(2))
+    centre, inverse_second = moments(group_spread(total(2), width))
 
     def second_row(row):
         at = pl.ds(row * cols, cols)
@@ -471,7 +473,7 @@
             at = pl.ds((start + p) * cols, cols)
             early = line * slope[at]
             sums.append((early, early * nfirst[at]))
-    share(3, gathered_sums(sums))
+    share(3, group_spread(gathered_sums(sums), width))
 
     for row in range(rows + 2):
         at = pl.ds(row * cols, cols)
@@ -540,7 +542,7 @@
         [jnp.sum(moved[3 * part : 3 * part + 3], axis=0, keepdims=True) for part in range(2)], axis=0
     )
 
-    spread = (group_spread(total(3), width) - moved) / cells
+    spread = (total(3) - moved) / cells
     for p in range(rows):
         at = pl.ds(p * cols, cols)
         back = gradient[p] * slope[at]

time: 21 us -> 20.5 us (0.976)
  Pallas kernels: 18.9 us -> 18.4 us
    pallas_call x1, Pallas kernels: 17.9 us -> 17.4 us  [body(): pl.pallas_call(functools.partial(kernel, n, m), out_shape=(jax.ShapeDtype...]
where the time goes in v6:
time: 20.5 us; the launch traced here: 20.4 us
  Pallas kernels  18.4 us (90%)
  between operations  1.93 us (9%)
    pallas_call x1, Pallas kernels, body(): pl.pallas_call(functools.partial(kernel, n, m), out_shape=(jax.ShapeDtype...  17.4 us
    pallas_call x1, Pallas kernels, body(): pl.pallas_call(finish, out_shape=(jax.ShapeDtypeStruct(images.shape, BF16...  1.04 us

profile of v6, /device:TPU:0, one launch (start us, length us, event | category | flops | bytes accessed | tf_op | source)
XLA Modules:
  0.0 20.4 jit_solution(15304676385896800251)
XLA Ops:
  1.9 17.4 %shard_map.156 = (bf16[1,4,64,256]{3,2,1,0:T(8,128)(2,1)S(1)}, bf16[1,4,64,256]{3,2,1,0:T(8,128)(2,1)S(1)}, bf16[32,256]{1,0:T(8,128)(2,1)S(1)}, bf16[32,512]{1,0:T(8,128)(2,1)S(1)}, f32[1,512]{1,0:T(1,128)S(1)}) custom-call(s32[1]{0:T(128)S(6)} %copy.17.steps_ref, s32[1]{0:T(128)S(6)} %copy.18.ids_ref, f32[1,256]{1,0:T(1,128)} %bitcast.6, ...), custom_call_target="tpu_custom_call" | custom-call | tf_op jit(solution)/shard_map/pallas_call | solution.py:612
  19.3 1.0 %shard_map.157 = (bf16[1,4,64,256]{3,2,1,0:T(8,128)(2,1)}, bf16[1,4,64,256]{3,2,1,0:T(8,128)(2,1)}, f32[256,512]{1,0:T(8,128)}, f32[1,512]{1,0:T(1,128)}) custom-call(bf16[1,4,64,256]{3,2,1,0:T(8,128)(2,1)S(1)} %get-tuple-element.13.branch, bf16[1,4,64,256]{3,2,1,0:T(8,128)(2,1)S(1)} %get-tuple-element.14.igrad, bf16[32,256]{1,0:T(8,128)(2,1)S(1)} %get-tuple-element.15.left, ...), custom_call_target="tpu_custom_call" | custom-call | tf_op jit(solution)/shard_map/pallas_call | solution.py:679

commit v7 on v6

--- a/solution.py
+++ b/solution.py
@@ -496,10 +496,12 @@
     def stacked(parts):
         if extra:
             parts = parts + [jnp.zeros((extra, parts[0].shape[1]), F32)]
-        return jnp.concatenate(parts, axis=0).astype(BF16)
+        return jnp.concatenate(parts, axis=0)
 
     thirds = [[piece.astype(F32) for piece in pieces(acts[k])] for k in range(m)]
-    left_out[...] = stacked([thirds[k][q] for q in (0, 0, 1, 0, 1, 2) for k in range(m)])
+    left_out[...] = stacked(
+        [thirds[k][q] for q in (0, 0, 1, 0, 1, 2) for k in range(m)]
+    ).T.astype(BF16)
 
     settle(2 * (n - 1), pair_recv.at[0])
 
@@ -555,7 +557,9 @@
         lines = [value[part : part + 1] for value in sums]
         thirds = [[piece.astype(F32) for piece in pieces(line)] for line in lines]
         columns = slice(part * channels, (part + 1) * channels)
-        right_out[:, columns] = stacked([thirds[k][q] for q in (0, 1, 0, 2, 1, 0) for k in range(m)])
+        right_out[:, columns] = stacked(
+            [thirds[k][q] for q in (0, 1, 0, 2, 1, 0) for k in range(m)]
+        ).astype(BF16)
         bgrad[:, columns] = add_up(lines)
 
     lines = 2 * (4 * (n - 1) + len(others)) + (m - 1) * acts.shape[2] // channels
@@ -584,10 +588,7 @@
     height = wgrad.shape[0] // PARTS
     for k in range(PARTS):
         at = pl.ds(k * height, height)
-        wgrad[at] = lax.dot_general(
-            left[:, k * height : (k + 1) * height], right[...],
-            (((0,), (0,)), ((), ())), preferred_element_type=F32,
-        )
+        wgrad[at] = jnp.dot(left[at], right[...], preferred_element_type=F32)
         copy = pltpu.make_async_copy(wgrad.at[at], wgrad_out.at[at], sem.at[3 + k])
         copy.start()
         copies.append(copy)
@@ -614,7 +615,7 @@
         out_shape=(
             jax.ShapeDtypeStruct(images.shape, BF16),
             jax.ShapeDtypeStruct(images.shape, BF16),
-            jax.ShapeDtypeStruct((stack, emb), BF16),
+            jax.ShapeDtypeStruct((emb, stack), BF16),
             jax.ShapeDtypeStruct((stack, 2 * channels), BF16),
             jax.ShapeDtypeStruct((1, 2 * channels), F32),
         ),

time: 20.5 us -> 20.5 us (level)
  no operation moved by 1% of the time
where the time goes in v7:
time: 20.5 us; the launch traced here: 20.3 us
  Pallas kernels  18.4 us (90%)
  between operations  1.93 us (9%)
    pallas_call x1, Pallas kernels, body(): pl.pallas_call(functools.partial(kernel, n, m), out_shape=(jax.ShapeDtype...  17.4 us
    pallas_call x1, Pallas kernels, body(): pl.pallas_call(finish, out_shape=(jax.ShapeDtypeStruct(images.shape, BF16...  0.99 us

profile of v7, /device:TPU:0, one launch (start us, length us, event | category | flops | bytes accessed | tf_op | source)
XLA Modules:
  0.0 20.3 jit_solution(12689360316447491204)
XLA Ops:
  1.9 17.4 %shard_map.156 = (bf16[1,4,64,256]{3,2,1,0:T(8,128)(2,1)S(1)}, bf16[1,4,64,256]{3,2,1,0:T(8,128)(2,1)S(1)}, bf16[256,32]{1,0:T(8,128)(2,1)S(1)}, bf16[32,512]{1,0:T(8,128)(2,1)S(1)}, f32[1,512]{1,0:T(1,128)S(1)}) custom-call(s32[1]{0:T(128)S(6)} %copy.17.steps_ref, s32[1]{0:T(128)S(6)} %copy.18.ids_ref, f32[1,256]{1,0:T(1,128)} %bitcast.6, ...), custom_call_target="tpu_custom_call" | custom-call | tf_op jit(solution)/shard_map/pallas_call | solution.py:613
  19.3 1.0 %shard_map.157 = (bf16[1,4,64,256]{3,2,1,0:T(8,128)(2,1)}, bf16[1,4,64,256]{3,2,1,0:T(8,128)(2,1)}, f32[256,512]{1,0:T(8,128)}, f32[1,512]{1,0:T(1,128)}) custom-call(bf16[1,4,64,256]{3,2,1,0:T(8,128)(2,1)S(1)} %get-tuple-element.13.branch, bf16[1,4,64,256]{3,2,1,0:T(8,128)(2,1)S(1)} %get-tuple-element.14.igrad, bf16[256,32]{1,0:T(8,128)(2,1)S(1)} %get-tuple-element.15.left, ...), custom_call_target="tpu_custom_call" | custom-call | tf_op jit(solution)/shard_map/pallas_call | solution.py:680
